TPU v7x, 256 devices: a whole 4x4x8 slice. The times are simulated.
256 devices in a mesh: dp: 32 (over x, z_lo, y), pipe: 8 (over z_hi, core).
Axes of the slice: x: 4, y: 4, z: 8 (z_hi: 4, z_lo: 2; z = z_hi * 2 + z_lo), core: 2. Of those that a mesh axis runs over, the one named last changes fastest.
Arguments:
- hidden_in: bfloat16 [32768, 2048], P(('dp', 'pipe')), may hold values from -24 to 24
- grad_out: bfloat16 [32768, 2048], P(('dp', 'pipe')), may hold values from -1.1953125 to 1.1953125
- w_query: bfloat16 [8, 2048, 512], P('pipe'), may hold values from -0.125 to 0.125
- w_key: bfloat16 [8, 2048, 512], P('pipe'), may hold values from -0.125 to 0.125
- w_value: bfloat16 [8, 2048, 512], P('pipe'), may hold values from -0.125 to 0.125
- w_out: bfloat16 [8, 512, 2048], P('pipe'), may hold values from -0.1875 to 0.1875
- pattern: int32 [4, 3], replicated, may hold values from 0 to 3, as said below
Outputs:
- hidden_out: bfloat16 [32768, 2048], P(('dp', 'pipe'))
- grad_in: bfloat16 [32768, 2048], P(('dp', 'pipe'))
- grad_query: float32 [8, 2048, 512], P('pipe', 'dp')
- grad_key: float32 [8, 2048, 512], P('pipe', 'dp')
- grad_value: float32 [8, 2048, 512], P('pipe', 'dp')
- grad_wout: float32 [8, 512, 2048], P('pipe', 'dp')
Inputs may be any that keep to these rules, and one draw needn't show every extreme that they name: `pattern`: row i lists key blocks for query block i: entry 0 is i, entry 1 is the block before i (i itself for the first block), the others are blocks no later than i; a row may repeat an entry.
All inputs are finite; a program needn't handle non-finite values.
Results may differ from a plain program's by a relative error of at most 0.023.
Values may be sent and summed in bfloat16 or wider, within the bound.
A program may use at most 128 MiB of HBM per device.

v0:
```python
import math

import jax
import jax.numpy as jnp
from jax import lax
from jax.sharding import PartitionSpec as P

HDIM = 64
BLK = 32


NORM_EPS = 1e-05


def partner(x, axis, apart):
    return lax.ppermute(x, axis, [(i, i ^ 1 << apart) for i in range(lax.axis_size(axis))])


def visible_mask(pattern, block_len):
    blocks, slot_count = pattern.shape
    equal_slot = pattern[:, :, None] == pattern[:, None, :]
    before = jnp.arange(slot_count)[None, :] < jnp.arange(slot_count)[:, None]
    repeated = jnp.any(equal_slot & before[None, :, :], axis=2)
    row_ids = jnp.arange(block_len)[:, None]
    column_ids = jnp.arange(block_len)[None, :]
    diagonal = pattern == jnp.arange(blocks, dtype=jnp.int32)[:, None]
    allowed = jnp.where(diagonal[:, :, None, None], (column_ids <= row_ids)[None, None], True)
    visible = allowed & jnp.logical_not(repeated)[:, :, None, None]
    return jnp.transpose(visible, (0, 2, 1, 3))


def contract(left_factor, right_factor):
    return lax.dot_general(
        left_factor, right_factor, (((0,), (0,)), ((), ())), preferred_element_type=jnp.float32
    )


def attend_forward(inputs, query_w, key_w, value_w, out_w, pattern, head_dim, block_len):
    amount, seq_len, features = inputs.shape
    blocks = seq_len // block_len
    head_count = query_w.shape[1] // head_dim
    input_f32 = inputs.astype(jnp.float32)
    factor = lax.rsqrt(jnp.mean(input_f32 * input_f32, axis=-1, keepdims=True) + NORM_EPS)
    normed = (input_f32 * factor).astype(jnp.bfloat16).reshape(amount * seq_len, features)
    query = jnp.dot(normed, query_w, preferred_element_type=jnp.float32).astype(jnp.bfloat16)
    key_proj = jnp.dot(normed, key_w, preferred_element_type=jnp.float32).astype(jnp.bfloat16)
    values = jnp.dot(normed, value_w, preferred_element_type=jnp.float32).astype(jnp.bfloat16)
    blocked = (amount, blocks, block_len, head_count, head_dim)
    query_blocks = query.reshape(blocked)
    keys_seen = jnp.take(key_proj.reshape(blocked), pattern, axis=1)
    values_seen = jnp.take(values.reshape(blocked), pattern, axis=1)
    inv_sqrt = 1.0 / math.sqrt(head_dim)
    scores = (
        jnp.einsum(
            "mqihd,mqsjhd->mqhisj", query_blocks, keys_seen, preferred_element_type=jnp.float32
        )
        * inv_sqrt
    )
    visible = visible_mask(pattern, block_len)[None, :, None]
    expo = jnp.where(visible, jnp.exp(scores), 0.0)
    totals = jnp.sum(expo, axis=(4, 5), keepdims=True)
    prob_f32 = expo / totals
    prob_bf16 = prob_f32.astype(jnp.bfloat16)
    attended = jnp.einsum(
        "mqhisj,mqsjhd->mqihd", prob_bf16, values_seen, preferred_element_type=jnp.float32
    )
    attended = attended.astype(jnp.bfloat16).reshape(amount * seq_len, head_count * head_dim)
    contrib = jnp.dot(attended, out_w, preferred_element_type=jnp.float32).astype(jnp.bfloat16)
    stash_fwd = (
        input_f32,
        factor,
        normed,
        query_blocks,
        keys_seen,
        values_seen,
        prob_f32,
        prob_bf16,
        attended,
    )
    return (contrib.reshape(amount, seq_len, features), stash_fwd)


def attend_backward(
    stash_fwd, cotangent, query_w, key_w, value_w, out_w, pattern, head_dim, block_len
):
    (
        input_f32,
        factor,
        normed,
        query_blocks,
        keys_seen,
        values_seen,
        prob_f32,
        prob_bf16,
        attended,
    ) = stash_fwd
    amount, seq_len, features = cotangent.shape
    blocks = seq_len // block_len
    head_count = query_w.shape[1] // head_dim
    inv_sqrt = 1.0 / math.sqrt(head_dim)
    grad_flat = cotangent.reshape(amount * seq_len, features)
    grad_attended = lax.dot_general(
        grad_flat, out_w, (((1,), (1,)), ((), ())), preferred_element_type=jnp.float32
    )
    grad_attended = grad_attended.astype(jnp.bfloat16).reshape(
        amount, blocks, block_len, head_count, head_dim
    )
    grad_prob = jnp.einsum(
        "mqihd,mqsjhd->mqhisj", grad_attended, values_seen, preferred_element_type=jnp.float32
    )
    grad_valseen = jnp.einsum(
        "mqhisj,mqihd->mqsjhd", prob_bf16, grad_attended, preferred_element_type=jnp.float32
    )
    inner_sum = jnp.sum(prob_f32 * grad_prob, axis=(4, 5), keepdims=True)
    grad_score = (prob_f32 * (grad_prob - inner_sum) * inv_sqrt).astype(jnp.bfloat16)
    grad_querypos = jnp.einsum(
        "mqhisj,mqsjhd->mqihd", grad_score, keys_seen, preferred_element_type=jnp.float32
    )
    grad_querypos = grad_querypos.astype(jnp.bfloat16).reshape(
        amount * seq_len, head_count * head_dim
    )
    grad_keyseen = jnp.einsum(
        "mqhisj,mqihd->mqsjhd", grad_score, query_blocks, preferred_element_type=jnp.float32
    )
    onehot = (pattern[:, :, None] == jnp.arange(blocks, dtype=jnp.int32)[None, None, :]).astype(
        jnp.float32
    )
    grad_keypos = jnp.einsum(
        "qsk,mqsjhd->mkjhd", onehot, grad_keyseen, precision=lax.Precision.HIGHEST
    )
    grad_keypos = grad_keypos.astype(jnp.bfloat16).reshape(amount * seq_len, head_count * head_dim)
    grad_valuepos = jnp.einsum(
        "qsk,mqsjhd->mkjhd", onehot, grad_valseen, precision=lax.Precision.HIGHEST
    )
    grad_valuepos = grad_valuepos.astype(jnp.bfloat16).reshape(
        amount * seq_len, head_count * head_dim
    )
    dims = (((1,), (1,)), ((), ()))
    grad_normed = lax.dot_general(grad_querypos, query_w, dims, preferred_element_type=jnp.float32)
    grad_normed = grad_normed + lax.dot_general(
        grad_keypos, key_w, dims, preferred_element_type=jnp.float32
    )
    grad_normed = grad_normed + lax.dot_general(
        grad_valuepos, value_w, dims, preferred_element_type=jnp.float32
    )
    grad_normed = grad_normed.reshape(amount, seq_len, features)
    mean_term = jnp.mean(input_f32 * grad_normed, axis=-1, keepdims=True)
    returned = (factor * grad_normed - input_f32 * factor * factor * factor * mean_term).astype(
        jnp.bfloat16
    )
    factor_pairs = (
        (normed, grad_querypos),
        (normed, grad_keypos),
        (normed, grad_valuepos),
        (attended, grad_flat),
    )
    return (returned, factor_pairs)


def on_device(hidden_in, grad_out, w_query, w_key, w_value, w_out, pattern):
    bit_count = lax.axis_size("pipe").bit_length() - 1
    bit_order = list(range(bit_count))
    query_w = w_query[0]
    key_w = w_key[0]
    value_w = w_value[0]
    out_w = w_out[0]

    def mirror_single(payload):
        for bit_index in bit_order:
            payload = partner(payload, "pipe", bit_index)
        return payload

    mirror_input = mirror_single(hidden_in)
    contrib, stash_fwd = attend_forward(
        jnp.stack([hidden_in, mirror_input]), query_w, key_w, value_w, out_w, pattern, HDIM, BLK
    )
    contrib_other = mirror_single(contrib[1])
    mirror_grad = mirror_single(grad_out)
    returned, factor_pairs = attend_backward(
        stash_fwd,
        jnp.stack([grad_out, mirror_grad]),
        query_w,
        key_w,
        value_w,
        out_w,
        pattern,
        HDIM,
        BLK,
    )
    returned_other = mirror_single(returned[1])
    hidden_out = (
        hidden_in.astype(jnp.float32)
        + contrib[0].astype(jnp.float32)
        + contrib_other.astype(jnp.float32)
    ).astype(jnp.bfloat16)
    grad_in = (
        grad_out.astype(jnp.float32)
        + returned[0].astype(jnp.float32)
        + returned_other.astype(jnp.float32)
    ).astype(jnp.bfloat16)
    full_grads = [contract(factor_pair[0], factor_pair[1]) for factor_pair in factor_pairs]
    shares = (
        lax.psum_scatter(
            full_grads[0].astype(jnp.bfloat16), "dp", scatter_dimension=0, tiled=True
        ).astype(jnp.float32),
        lax.psum_scatter(
            full_grads[1].astype(jnp.bfloat16), "dp", scatter_dimension=0, tiled=True
        ).astype(jnp.float32),
        lax.psum_scatter(
            full_grads[2].astype(jnp.bfloat16), "dp", scatter_dimension=0, tiled=True
        ).astype(jnp.float32),
        lax.psum_scatter(
            full_grads[3].astype(jnp.bfloat16), "dp", scatter_dimension=0, tiled=True
        ).astype(jnp.float32),
    )
    return (hidden_out, grad_in, shares[0][None], shares[1][None], shares[2][None], shares[3][None])


def solution(mesh):
    in_specs = (
        P(("dp", "pipe"), None),
        P(("dp", "pipe"), None),
        P("pipe", None, None),
        P("pipe", None, None),
        P("pipe", None, None),
        P("pipe", None, None),
        P(),
    )
    out_specs = (
        P(("dp", "pipe"), None),
        P(("dp", "pipe"), None),
        P("pipe", "dp", None),
        P("pipe", "dp", None),
        P("pipe", "dp", None),
        P("pipe", "dp", None),
    )
    return jax.shard_map(
        on_device, mesh=mesh, in_specs=in_specs, out_specs=out_specs, check_vma=False
    )
```

profile of v0, /device:TPU:64, one launch (start us, length us, event | category | flops | bytes accessed | tf_op | source)
XLA Modules:
  0.0 889.5 jit_solution(13449413906516051888)
XLA Ops:
  9.4 1.4 collective-permute-start.1
  11.6 1.6 collective-permute-start.7
  14.1 31.1 %collective-permute-done.1 = bf16[128,2048]{1,0:T(8,128)(2,1)} collective-permute-done((bf16[128,2048]{1,0:T(8,128)(2,1)S(1)}, bf16[128,2048]{1,0:T(8,128)(2,1)}, u32[]{:S(2)}, u32[]{:S(2)}) %collective-permute-start.1) | collective-permute-done | bytes 524320 | tf_op jit(solution)/shard_map/ppermute | solution.py:16
  45.1 5.7 collective-permute-start.2
  51.5 16.0 %collective-permute-done.7 = bf16[128,2048]{1,0:T(8,128)(2,1)} collective-permute-done((bf16[128,2048]{1,0:T(8,128)(2,1)S(1)}, bf16[128,2048]{1,0:T(8,128)(2,1)}, u32[]{:S(2)}, u32[]{:S(2)}) %collective-permute-start.7) | collective-permute-done | bytes 524320 | tf_op jit(solution)/shard_map/ppermute | solution.py:16
  67.5 5.6 collective-permute-start.8
  73.3 11.8 %collective-permute-done.2 = bf16[128,2048]{1,0:T(8,128)(2,1)S(1)} collective-permute-done((bf16[128,2048]{1,0:T(8,128)(2,1)}, bf16[128,2048]{1,0:T(8,128)(2,1)S(1)}, u32[]{:S(2)}, u32[]{:S(2)}) %collective-permute-start.2) | collective-permute-done | bytes 524320 | tf_op jit(solution)/shard_map/ppermute | solution.py:16
  85.1 1.5 multiply_reduce_fusion.1
  86.6 9.7 %collective-permute-done.8 = bf16[128,2048]{1,0:T(8,128)(2,1)S(1)} collective-permute-done((bf16[128,2048]{1,0:T(8,128)(2,1)}, bf16[128,2048]{1,0:T(8,128)(2,1)S(1)}, u32[]{:S(2)}, u32[]{:S(2)}) %collective-permute-start.8) | collective-permute-done | bytes 524320 | tf_op jit(solution)/shard_map/ppermute | solution.py:16
  100.3 1.6 multiply_convert_fusion.1
  104.0 2.3 fusion.45
  109.1 3.0 gather_fusion
  112.1 3.0 gather_fusion.1
  115.1 2.2 select_bitcast_fusion.1
  122.6 2.4 multiply_convert_fusion
  126.3 5.0 fusion.34
  132.1 1.4 reshape.270
  133.5 2.1 convolution_convert_fusion.2
  135.7 2.1 fusion.56
  137.8 4.8 fusion.37
  143.4 1.4 reshape.271
  144.8 2.0 convolution_convert_fusion.1
  146.9 2.4 fusion.41
  150.4 1.4 reshape.266
  151.8 3.3 convolution_convert_fusion
  155.4 2.4 fusion.40
  158.9 2.1 reshape.269
  161.0 2.3 convolution_convert_fusion.4
  165.2 2.1 convolution_convert_fusion.3
  167.3 2.5 fusion.13
  171.1 2.2 fusion.6
  173.3 2.3 subtract_convert_fusion
  176.2 21.0 %collective-permute-start.4 = (bf16[128,2048]{1,0:T(8,128)(2,1)}, bf16[128,2048]{1,0:T(8,128)(2,1)S(1)}, u32[]{:S(2)}, u32[]{:S(2)}) collective-permute-start(bf16[128,2048]{1,0:T(8,128)(2,1)} %collective-permute-done.3), channel_id=1, source_target_pairs={{0,2},{1,3},{2,0},{3,1},{4,6},{5,7},{6,4},{7,5},{8,10},{9,11},{10,... | collective-permute-start | bytes 1572872 | tf_op jit(solution)/shard_map/ppermute | solution.py:16
  197.2 1.5 collective-permute-start.10
  198.8 40.8 %collective-permute-done.4 = bf16[128,2048]{1,0:T(8,128)(2,1)S(1)} collective-permute-done((bf16[128,2048]{1,0:T(8,128)(2,1)}, bf16[128,2048]{1,0:T(8,128)(2,1)S(1)}, u32[]{:S(2)}, u32[]{:S(2)}) %collective-permute-start.4) | collective-permute-done | bytes 524320 | tf_op jit(solution)/shard_map/ppermute | solution.py:16
  239.6 16.1 %collective-permute-start.5 = (bf16[128,2048]{1,0:T(8,128)(2,1)S(1)}, bf16[128,2048]{1,0:T(8,128)(2,1)S(1)}, u32[]{:S(2)}, u32[]{:S(2)}) collective-permute-start(bf16[128,2048]{1,0:T(8,128)(2,1)S(1)} %collective-permute-done.4), channel_id=1, source_target_pairs={{0,4},{1,5},{2,6},{3,7},{4,0},{5,1},{6,2},{7,3},{8,12},{9,13},{10,... | collective-permute-start | bytes 1572872 | tf_op jit(solution)/shard_map/ppermute | solution.py:16
  255.7 6.2 collective-permute-done.10
  261.9 4.9 collective-permute-start.11
  266.7 28.3 %collective-permute-done.5 = bf16[128,2048]{1,0:T(8,128)(2,1)S(1)} collective-permute-done((bf16[128,2048]{1,0:T(8,128)(2,1)S(1)}, bf16[128,2048]{1,0:T(8,128)(2,1)S(1)}, u32[]{:S(2)}, u32[]{:S(2)}) %collective-permute-start.5) | collective-permute-done | bytes 524320 | tf_op jit(solution)/shard_map/ppermute | solution.py:16
  296.1 11.5 %collective-permute-done.11 = bf16[128,2048]{1,0:T(8,128)(2,1)S(1)} collective-permute-done((bf16[128,2048]{1,0:T(8,128)(2,1)S(1)}, bf16[128,2048]{1,0:T(8,128)(2,1)S(1)}, u32[]{:S(2)}, u32[]{:S(2)}) %collective-permute-start.11) | collective-permute-done | bytes 524320 | tf_op jit(solution)/shard_map/ppermute | solution.py:16
  308.6 63.5 %reduce-scatter.7.cloned.1.call-done = bf16[64,512]{1,0:T(8,128)(2,1)} async-done(((bf16[2048,512]{1,0:T(8,128)(2,1)}), bf16[64,512]{1,0:T(8,128)(2,1)}) %reduce-scatter.7.cloned.1.call-update) | async-done | bytes 65552 | tf_op jit(solution)/shard_map/reduce_scatter | solution.py:206
  372.1 1.5 bitcast_convert_fusion.2
  373.7 176.3 %reduce-scatter.9.cloned.1.call-done = bf16[64,512]{1,0:T(8,128)(2,1)} async-done(((bf16[2048,512]{1,0:T(8,128)(2,1)}), bf16[64,512]{1,0:T(8,128)(2,1)}) %reduce-scatter.9.cloned.1.call-update) | async-done | bytes 65552 | tf_op jit(solution)/shard_map/reduce_scatter | solution.py:209
  549.9 1.5 bitcast_convert_fusion.1
  551.4 164.5 %reduce-scatter.11.cloned.1.call-done = bf16[16,2048]{1,0:T(8,128)(2,1)} async-done(((bf16[512,2048]{1,0:T(8,128)(2,1)}), bf16[16,2048]{1,0:T(8,128)(2,1)}) %reduce-scatter.11.cloned.1.call-update) | async-done | bytes 65552 | tf_op jit(solution)/shard_map/reduce_scatter | solution.py:212
  715.9 1.5 bitcast_convert_fusion
  717.4 164.0 %reduce-scatter.5.cloned.1.call-done = bf16[64,512]{1,0:T(8,128)(2,1)} async-done(((bf16[2048,512]{1,0:T(8,128)(2,1)}), bf16[64,512]{1,0:T(8,128)(2,1)}) %reduce-scatter.5.cloned.1.call-update) | async-done | bytes 65552 | tf_op jit(solution)/shard_map/reduce_scatter | solution.py:203
  881.5 1.5 bitcast_convert_fusion.3
  (97 shorter events, 30.2 us)
Async XLA Ops:
  7.2 100.2 %copy-start = (bf16[1,2048,512]{2,1,0:T(8,128)(2,1)S(1)}, bf16[1,2048,512]{2,1,0:T(8,128)(2,1)}, u32[]{:S(2)}) copy-start(bf16[1,2048,512]{2,1,0:T(8,128)(2,1)} %param.13) | copy-start | bytes 6291460
  7.2 365.0 %reduce-scatter.7.cloned.1.call-start = ((), (), s32[]{:S(2)}) async-start(), calls=%async_computation.5 | async-start | bytes 2162688 | tf_op jit(solution)/shard_map/reduce_scatter | solution.py:206
  7.2 2.2 collective-permute-start
  7.3 4.2 collective-permute-start.6
  9.4 35.7 %collective-permute-start.1 = (bf16[128,2048]{1,0:T(8,128)(2,1)S(1)}, bf16[128,2048]{1,0:T(8,128)(2,1)}, u32[]{:S(2)}, u32[]{:S(2)}) collective-permute-start(bf16[128,2048]{1,0:T(8,128)(2,1)S(1)} %collective-permute-done), channel_id=1, source_target_pairs={{0,2},{1,3},{2,0},{3,1},{4,6},{5,7},{6,4},{7,5},{8,10},{9,11},{10,... | collective-permute-start | bytes 1572872 | tf_op jit(solution)/shard_map/ppermute | solution.py:16
  11.6 55.9 %collective-permute-start.7 = (bf16[128,2048]{1,0:T(8,128)(2,1)S(1)}, bf16[128,2048]{1,0:T(8,128)(2,1)}, u32[]{:S(2)}, u32[]{:S(2)}) collective-permute-start(bf16[128,2048]{1,0:T(8,128)(2,1)S(1)} %collective-permute-done.6), channel_id=1, source_target_pairs={{0,2},{1,3},{2,0},{3,1},{4,6},{5,7},{6,4},{7,5},{8,10},{9,11},{10,... | collective-permute-start | bytes 1572872 | tf_op jit(solution)/shard_map/ppermute | solution.py:16
  45.1 40.0 %collective-permute-start.2 = (bf16[128,2048]{1,0:T(8,128)(2,1)}, bf16[128,2048]{1,0:T(8,128)(2,1)S(1)}, u32[]{:S(2)}, u32[]{:S(2)}) collective-permute-start(bf16[128,2048]{1,0:T(8,128)(2,1)} %collective-permute-done.1), channel_id=1, source_target_pairs={{0,4},{1,5},{2,6},{3,7},{4,0},{5,1},{6,2},{7,3},{8,12},{9,13},{10,... | collective-permute-start | bytes 1572872 | tf_op jit(solution)/shard_map/ppermute | solution.py:16
  67.5 28.9 %collective-permute-start.8 = (bf16[128,2048]{1,0:T(8,128)(2,1)}, bf16[128,2048]{1,0:T(8,128)(2,1)S(1)}, u32[]{:S(2)}, u32[]{:S(2)}) collective-permute-start(bf16[128,2048]{1,0:T(8,128)(2,1)} %collective-permute-done.7), channel_id=1, source_target_pairs={{0,4},{1,5},{2,6},{3,7},{4,0},{5,1},{6,2},{7,3},{8,12},{9,13},{10,... | collective-permute-start | bytes 1572872 | tf_op jit(solution)/shard_map/ppermute | solution.py:16
  73.2 25.3 %copy-start.20 = (bf16[1,512,2048]{2,1,0:T(8,128)(2,1)S(1)}, bf16[1,512,2048]{2,1,0:T(8,128)(2,1)}, u32[]{:S(2)}) copy-start(bf16[1,512,2048]{2,1,0:T(8,128)(2,1)} %param.14) | copy-start | bytes 6291460
  85.1 14.1 %copy-start.5 = (bf16[128,2048]{1,0:T(8,128)(2,1)}, bf16[128,2048]{1,0:T(8,128)(2,1)S(1)}, u32[]{:S(2)}) copy-start(bf16[128,2048]{1,0:T(8,128)(2,1)S(1)} %collective-permute-done.2) | copy-start | bytes 1572868
  97.5 1.0 copy-start.11
  100.3 1.9 copy-start.18
  117.3 1.1 copy-start.2
  117.3 1.6 copy-start.3
  117.7 1.4 copy-start.7
  119.1 1.0 copy-start.8
  125.0 1.2 copy-start.1
  133.5 2.1 copy-start.12
  135.6 414.3 %reduce-scatter.9.cloned.1.call-start = ((), (), s32[]{:S(2)}) async-start(), calls=%async_computation.6 | async-start | bytes 2162688 | tf_op jit(solution)/shard_map/reduce_scatter | solution.py:209
  144.8 2.1 copy-start.14
  146.9 569.1 %reduce-scatter.11.cloned.1.call-start = ((), (), s32[]{:S(2)}) async-start(), calls=%async_computation.7 | async-start | bytes 2162688 | tf_op jit(solution)/shard_map/reduce_scatter | solution.py:212
  155.1 726.4 %reduce-scatter.5.cloned.1.call-start = ((), (), s32[]{:S(2)}) async-start(), calls=%async_computation.4 | async-start | bytes 2162688 | tf_op jit(solution)/shard_map/reduce_scatter | solution.py:203
  161.0 4.2 copy-start.16
  163.3 1.0 copy-start.9
  165.2 2.1 copy-start.17
  165.2 11.1 %collective-permute-start.3 = (bf16[128,2048]{1,0:T(8,128)(2,1)}, bf16[128,2048]{1,0:T(8,128)(2,1)}, u32[]{:S(2)}, u32[]{:S(2)}) collective-permute-start(bf16[128,2048]{1,0:T(8,128)(2,1)} %slice.23), channel_id=1, source_target_pairs={{0,1},{1,0},{2,3},{3,2},{4,5},{5,4},{6,7},{7,6},{8,9},{9,8},{10,11... | collective-permute-start | bytes 1572872 | tf_op jit(solution)/shard_map/ppermute | solution.py:16
  167.3 2.5 copy-start.13
  167.3 2.5 copy-start.19
  169.8 1.0 copy-start.4
  169.8 1.2 copy-start.6
  169.8 1.2 copy-start.15
  173.3 121.8 %copy-start.10 = (bf16[256,2048]{1,0:T(8,128)(2,1)S(1)}, bf16[256,2048]{1,0:T(8,128)(2,1)}, u32[]{:S(2)}) copy-start(bf16[256,2048]{1,0:T(8,128)(2,1)} %copy-done.9) | copy-start | bytes 3145732
  175.6 132.0 %copy-start.21 = (bf16[128,2048]{1,0:T(8,128)(2,1)S(1)}, bf16[128,2048]{1,0:T(8,128)(2,1)}, u32[]{:S(2)}) copy-start(bf16[128,2048]{1,0:T(8,128)(2,1)} %param.10) | copy-start | bytes 1572868
  175.6 21.6 %collective-permute-start.9 = (bf16[128,2048]{1,0:T(8,128)(2,1)S(1)}, bf16[128,2048]{1,0:T(8,128)(2,1)S(1)}, u32[]{:S(2)}, u32[]{:S(2)}) collective-permute-start(bf16[128,2048]{1,0:T(8,128)(2,1)S(1)} %slice_bitcast_fusion), channel_id=1, source_target_pairs={{0,1},{1,0},{2,3},{3,2},{4,5},{5,4},{6,7},{7,6},{8,9},{9,8},{10,11... | collective-permute-start | bytes 1572872 | tf_op jit(solution)/shard_map/ppermute | solution.py:16
  176.2 63.4 %collective-permute-start.4 = (bf16[128,2048]{1,0:T(8,128)(2,1)}, bf16[128,2048]{1,0:T(8,128)(2,1)S(1)}, u32[]{:S(2)}, u32[]{:S(2)}) collective-permute-start(bf16[128,2048]{1,0:T(8,128)(2,1)} %collective-permute-done.3), channel_id=1, source_target_pairs={{0,2},{1,3},{2,0},{3,1},{4,6},{5,7},{6,4},{7,5},{8,10},{9,11},{10,... | collective-permute-start | bytes 1572872 | tf_op jit(solution)/shard_map/ppermute | solution.py:16
  197.2 64.6 %collective-permute-start.10 = (bf16[128,2048]{1,0:T(8,128)(2,1)S(1)}, bf16[128,2048]{1,0:T(8,128)(2,1)S(1)}, u32[]{:S(2)}, u32[]{:S(2)}) collective-permute-start(bf16[128,2048]{1,0:T(8,128)(2,1)S(1)} %collective-permute-done.9), channel_id=1, source_target_pairs={{0,2},{1,3},{2,0},{3,1},{4,6},{5,7},{6,4},{7,5},{8,10},{9,11},{10,... | collective-permute-start | bytes 1572872 | tf_op jit(solution)/shard_map/ppermute | solution.py:16
  239.6 55.5 %collective-permute-start.5 = (bf16[128,2048]{1,0:T(8,128)(2,1)S(1)}, bf16[128,2048]{1,0:T(8,128)(2,1)S(1)}, u32[]{:S(2)}, u32[]{:S(2)}) collective-permute-start(bf16[128,2048]{1,0:T(8,128)(2,1)S(1)} %collective-permute-done.4), channel_id=1, source_target_pairs={{0,4},{1,5},{2,6},{3,7},{4,0},{5,1},{6,2},{7,3},{8,12},{9,13},{10,... | collective-permute-start | bytes 1572872 | tf_op jit(solution)/shard_map/ppermute | solution.py:16
  261.9 45.7 %collective-permute-start.11 = (bf16[128,2048]{1,0:T(8,128)(2,1)S(1)}, bf16[128,2048]{1,0:T(8,128)(2,1)S(1)}, u32[]{:S(2)}, u32[]{:S(2)}) collective-permute-start(bf16[128,2048]{1,0:T(8,128)(2,1)S(1)} %collective-permute-done.10), channel_id=1, source_target_pairs={{0,4},{1,5},{2,6},{3,7},{4,0},{5,1},{6,2},{7,3},{8,12},{9,13},{10,... | collective-permute-start | bytes 1572872 | tf_op jit(solution)/shard_map/ppermute | solution.py:16
Sparse Core Ops, SparseCore 0:
  135.7 236.3 reduce-scatter.6
  374.7 175.2 reduce-scatter.8
  552.4 163.4 reduce-scatter.10
  718.3 163.1 reduce-scatter.4
where the time goes:
time: 891 us; the launch traced here: 890 us
  waiting for transfers between devices  725 us (81%)
  starting transfers between devices  59.3 us (7%)
  matrix products  40.1 us (5%)
  local copies, waits for them, and re-layouts  27.8 us (3%)
  other arithmetic  23.5 us (3%)
  between operations  14.1 us (2%)
    reduce_scatter x1, waiting for transfers between devices, on_device(): lax.psum_scatter(full_grads[2].astype(jnp.bfloat16), 'dp', scatter_dimens...  176 us
    reduce_scatter x1, waiting for transfers between devices, on_device(): lax.psum_scatter(full_grads[3].astype(jnp.bfloat16), 'dp', scatter_dimens...  165 us
    reduce_scatter x1, waiting for transfers between devices, on_device(): lax.psum_scatter(full_grads[0].astype(jnp.bfloat16), 'dp', scatter_dimens...  164 us
    ppermute x12, waiting for transfers between devices, partner(): lax.ppermute(x, axis, [(i, i ^ 1 << apart) for i in range(lax.axis_size(a...  156 us
    reduce_scatter x1, waiting for transfers between devices, on_device(): lax.psum_scatter(full_grads[1].astype(jnp.bfloat16), 'dp', scatter_dimens...  63.5 us
    ppermute x12, starting transfers between devices, partner(): lax.ppermute(x, axis, [(i, i ^ 1 << apart) for i in range(lax.axis_size(a...  58.9 us
  transfers between devices with their start and end apart: 16, of which 13 were waited for; matrix products, arithmetic and copies ran while one was open for 6% of the time, Pallas kernels for 0%

commit v1 on v0

--- a/solution.py
+++ b/solution.py
@@ -3,6 +3,8 @@
 import jax
 import jax.numpy as jnp
 from jax import lax
+from jax.experimental import pallas as pl
+from jax.experimental.pallas import tpu as pltpu
 from jax.sharding import PartitionSpec as P
 
 HDIM = 64
@@ -12,8 +14,134 @@
 NORM_EPS = 1e-05
 
 
-def partner(x, axis, apart):
-    return lax.ppermute(x, axis, [(i, i ^ 1 << apart) for i in range(lax.axis_size(axis))])
+MESH = pl.DeviceIdType.MESH
+X_SIZE, Z_SIZE, Y_SIZE = 4, 2, 4
+
+
+def ring_scatter_kernel(*refs):
+    count = 4
+    parts = refs[:count]
+    outs = refs[count : 2 * count]
+    scratch = refs[2 * count :]
+    far, near, far2, near2, last = (scratch[i * count : (i + 1) * count] for i in range(5))
+    send_sem, recv_sem = scratch[5 * count], scratch[5 * count + 1]
+    dp = lax.axis_index("dp")
+    pipe = lax.axis_index("pipe")
+    x_at = dp // (Z_SIZE * Y_SIZE)
+    z_at = lax.rem(dp // Y_SIZE, Z_SIZE)
+    y_at = lax.rem(dp, Y_SIZE)
+
+    def device(x, z, y):
+        return ((x * Z_SIZE + z) * Y_SIZE + y, pipe)
+
+    def x_to(step):
+        return device(lax.rem(x_at + step, X_SIZE), z_at, y_at)
+
+    def y_to(step):
+        return device(x_at, z_at, lax.rem(y_at + step, Y_SIZE))
+
+    mate = device(x_at, 1 - z_at, y_at)
+    barrier = pltpu.get_barrier_semaphore()
+    for target in (x_to(1), x_to(3), y_to(1), y_to(3), mate):
+        pl.semaphore_signal(barrier, inc=1, device_id=target, device_id_type=MESH)
+    pl.semaphore_wait(barrier, 5)
+
+    x_first = (True, True, False, False)
+    order = (0, 2, 1, 3)
+    started = []
+
+    def copy(src, dst, t, slot, target):
+        made = pltpu.make_async_remote_copy(
+            src_ref=src,
+            dst_ref=dst,
+            send_sem=send_sem.at[t, slot],
+            recv_sem=recv_sem.at[t, slot],
+            device_id=target,
+            device_id_type=MESH,
+        )
+        made.start()
+        started.append(made)
+        return made
+
+    def total(*terms):
+        acc = terms[0].astype(jnp.float32)
+        for term in terms[1:]:
+            acc = acc + term.astype(jnp.float32)
+        return acc
+
+    def ring(stage, base, take, here, send_to, far_bufs, near_bufs):
+        msgs = {}
+        for t in order:
+            at = here[t]
+            opposite = lax.rem(at + 2, 4)
+            msgs[t, 0] = copy(take(t, opposite, 0), far_bufs[t].at[0], t, base, send_to(t, 1))
+            msgs[t, 1] = copy(take(t, opposite, 1), far_bufs[t].at[1], t, base + 1, send_to(t, 3))
+        for t in order:
+            right, left = lax.rem(here[t] + 1, 4), lax.rem(here[t] + 3, 4)
+            msgs[t, 2] = copy(take(t, right, 1), near_bufs[t].at[0, 1], t, base + 2, send_to(t, 1))
+            msgs[t, 3] = copy(take(t, left, 0), near_bufs[t].at[1, 0], t, base + 3, send_to(t, 3))
+        for t in order:
+            right, left = lax.rem(here[t] + 1, 4), lax.rem(here[t] + 3, 4)
+            msgs[t, 0].wait_recv()
+            far_bufs[t][0] = total(take(t, right, 0)[...], far_bufs[t][0]).astype(jnp.bfloat16)
+            msgs[t, 4] = copy(far_bufs[t].at[0], near_bufs[t].at[0, 0], t, base + 4, send_to(t, 1))
+            msgs[t, 1].wait_recv()
+            far_bufs[t][1] = total(take(t, left, 1)[...], far_bufs[t][1]).astype(jnp.bfloat16)
+            msgs[t, 5] = copy(far_bufs[t].at[1], near_bufs[t].at[1, 1], t, base + 5, send_to(t, 3))
+        return msgs
+
+    def take_first(t, at, z):
+        return parts[t].at[at, z] if x_first[t] else parts[t].at[:, z, at]
+
+    def take_second(t, at, z):
+        return near[t].at[0, z, at]
+
+    first_at = [x_at if first else y_at for first in x_first]
+    second_at = [y_at if first else x_at for first in x_first]
+    msgs = ring(0, 0, take_first, first_at, lambda t, s: x_to(s) if x_first[t] else y_to(s), far, near)
+    for t in order:
+        for slot in range(2, 6):
+            msgs[t, slot].wait_recv()
+        for z in range(2):
+            own = take_first(t, first_at[t], z)[...]
+            near[t][0, z] = total(own, near[t][0, z], near[t][1, z]).astype(jnp.bfloat16)
+    msgs = ring(1, 6, take_second, second_at, lambda t, s: y_to(s) if x_first[t] else x_to(s), far2, near2)
+    finals = {}
+    for t in order:
+        for slot in range(2, 6):
+            msgs[t, slot].wait_recv()
+        for z in range(2):
+            own = take_second(t, second_at[t], z)[...]
+            near2[t][0, z] = total(own, near2[t][0, z], near2[t][1, z]).astype(jnp.bfloat16)
+        finals[t] = copy(near2[t].at[0, 1 - z_at], last[t], t, 12, mate)
+    for t in order:
+        finals[t].wait_recv()
+        outs[t][...] = total(near2[t][0, z_at], last[t][...])
+    for made in started:
+        made.wait_send()
+
+
+def ring_scatter(parts):
+    split = [p.reshape(X_SIZE, Z_SIZE, Y_SIZE, p.shape[0] // 32, p.shape[1]) for p in parts]
+    tails = [p.shape[3:] for p in split]
+    vmem = pl.BlockSpec(memory_space=pltpu.VMEM)
+    bf16 = jnp.bfloat16
+    return pl.pallas_call(
+        ring_scatter_kernel,
+        out_shape=tuple(jax.ShapeDtypeStruct(t, jnp.float32) for t in tails),
+        in_specs=[vmem] * 4,
+        out_specs=(vmem,) * 4,
+        scratch_shapes=[pltpu.VMEM((2, 4) + t, bf16) for t in tails]
+        + [pltpu.VMEM((2, 2, 4) + t, bf16) for t in tails]
+        + [pltpu.VMEM((2,) + t, bf16) for t in tails]
+        + [pltpu.VMEM((2, 2) + t, bf16) for t in tails]
+        + [pltpu.VMEM(t, bf16) for t in tails]
+        + [pltpu.SemaphoreType.DMA((4, 13)), pltpu.SemaphoreType.DMA((4, 13))],
+        compiler_params=pltpu.CompilerParams(
+            collective_id=0, has_side_effects=True, vmem_limit_bytes=40 * 1024 * 1024
+        ),
+        name="ring_scatter",
+    )(*split)
 
 
 def visible_mask(pattern, block_len):
@@ -158,17 +286,14 @@
 
 
 def on_device(hidden_in, grad_out, w_query, w_key, w_value, w_out, pattern):
-    bit_count = lax.axis_size("pipe").bit_length() - 1
-    bit_order = list(range(bit_count))
     query_w = w_query[0]
     key_w = w_key[0]
     value_w = w_value[0]
     out_w = w_out[0]
 
     def mirror_single(payload):
-        for bit_index in bit_order:
-            payload = partner(payload, "pipe", bit_index)
-        return payload
+        slots = lax.axis_size("pipe")
+        return lax.ppermute(payload, "pipe", [(i, slots - 1 - i) for i in range(slots)])
 
     mirror_input = mirror_single(hidden_in)
     contrib, stash_fwd = attend_forward(
@@ -199,20 +324,7 @@
         + returned_other.astype(jnp.float32)
     ).astype(jnp.bfloat16)
     full_grads = [contract(factor_pair[0], factor_pair[1]) for factor_pair in factor_pairs]
-    shares = (
-        lax.psum_scatter(
-            full_grads[0].astype(jnp.bfloat16), "dp", scatter_dimension=0, tiled=True
-        ).astype(jnp.float32),
-        lax.psum_scatter(
-            full_grads[1].astype(jnp.bfloat16), "dp", scatter_dimension=0, tiled=True
-        ).astype(jnp.float32),
-        lax.psum_scatter(
-            full_grads[2].astype(jnp.bfloat16), "dp", scatter_dimension=0, tiled=True
-        ).astype(jnp.float32),
-        lax.psum_scatter(
-            full_grads[3].astype(jnp.bfloat16), "dp", scatter_dimension=0, tiled=True
-        ).astype(jnp.float32),
-    )
+    shares = ring_scatter([full.astype(jnp.bfloat16) for full in full_grads])
     return (hidden_out, grad_in, shares[0][None], shares[1][None], shares[2][None], shares[3][None])
 
 

time: 891 us -> 191 us (0.21)
  the two profiles are of different devices: /device:TPU:64 before, /device:TPU:1 now
where the time goes in v1:
time: 191 us; the launch traced here: 190 us
  Pallas kernels  54 us (28%)
  waiting for transfers between devices  40.7 us (21%)
  local copies, waits for them, and re-layouts  33.4 us (17%)
  matrix products  31.9 us (17%)
  other arithmetic  17 us (9%)
  starting transfers between devices  12.2 us (6%)
    pallas_call x1, Pallas kernels, ring_scatter(): pl.pallas_call(ring_scatter_kernel, out_shape=tuple((jax.ShapeDtypeStruct...  54 us
    ppermute x4, waiting for transfers between devices, mirror_single(): lax.ppermute(payload, 'pipe', [(i, slots - 1 - i) for i in range(slots)])  40.7 us
    ppermute x4, starting transfers between devices, mirror_single(): lax.ppermute(payload, 'pipe', [(i, slots - 1 - i) for i in range(slots)])  12.2 us
    unnamed x47, local copies, waits for them, and re-layouts  9.65 us
    dot_general x4, matrix products, contract(): lax.dot_general(left_factor, right_factor, (((0,), (0,)), ((), ())), pref...  5.38 us
    unnamed x4, matrix products  5.21 us
    dot_general x1, matrix products, attend_backward(): jnp.einsum('qsk,mqsjhd->mkjhd', onehot, grad_valseen, precision=lax.Preci...  4.79 us
    dot_general x1, matrix products, attend_backward(): jnp.einsum('qsk,mqsjhd->mkjhd', onehot, grad_keyseen, precision=lax.Preci...  4.79 us
  transfers between devices with their start and end apart: 4, of which 2 were waited for; matrix products, arithmetic and copies ran while one was open for 17% of the time, Pallas kernels for 28%

profile of v1, /device:TPU:1, one launch (start us, length us, event | category | flops | bytes accessed | tf_op | source)
XLA Modules:
  0.0 190.2 jit_solution(15122278836580676211)
XLA Ops:
  0.6 7.5 %collective-permute-start = (bf16[128,2048]{1,0:T(8,128)(2,1)}, bf16[128,2048]{1,0:T(8,128)(2,1)S(1)}, u32[]{:S(2)}, u32[]{:S(2)}) collective-permute-start(bf16[128,2048]{1,0:T(8,128)(2,1)} %param.9), channel_id=1, source_target_pairs={{0,7},{1,6},{2,5},{3,4},{4,3},{5,2},{6,1},{7,0},{8,15},{9,14},{10,... | collective-permute-start | bytes 1572872 | tf_op jit(solution)/shard_map/ppermute | solution.py:296
  8.2 0.8 copy.31
  9.8 0.9 and_reduce_fusion
  11.6 31.0 %collective-permute-done = bf16[128,2048]{1,0:T(8,128)(2,1)S(1)} collective-permute-done((bf16[128,2048]{1,0:T(8,128)(2,1)}, bf16[128,2048]{1,0:T(8,128)(2,1)S(1)}, u32[]{:S(2)}, u32[]{:S(2)}) %collective-permute-start) | collective-permute-done | bytes 524320 | tf_op jit(solution)/shard_map/ppermute | solution.py:296
  42.6 1.5 multiply_reduce_fusion.1
  44.2 9.7 %collective-permute-done.2 = bf16[128,2048]{1,0:T(8,128)(2,1)S(1)} collective-permute-done((bf16[128,2048]{1,0:T(8,128)(2,1)}, bf16[128,2048]{1,0:T(8,128)(2,1)S(1)}, u32[]{:S(2)}, u32[]{:S(2)}) %collective-permute-start.2) | collective-permute-done | bytes 524320 | tf_op jit(solution)/shard_map/ppermute | solution.py:296
  53.9 1.1 pad_maximum_fusion.1
  55.0 1.0 copy-done.12
  56.0 0.7 fusion.51
  56.8 1.1 reshape.280
  57.8 1.6 multiply_convert_fusion.1
  60.5 1.1 reshape.277
  61.6 2.3 %fusion.45 = bf16[256,512]{1,0:T(8,128)(2,1)S(1)} fusion(bf16[256,2048]{1,0:T(8,128)(2,1)S(1)} %bitcast.164, bf16[1,2048,512]{2,1,0:T(8,128)(2,1)} %param.11), kind=kOutput, calls=%fused_computation.51 | convolution fusion | flops 537001984 | bytes 3407872 | tf_op jit(solution)/shard_map/dot_general | solution.py:173
  63.9 1.1 reshape.276
  65.6 1.1 reshape.275
  66.7 3.0 %gather_fusion = bf16[12,2,32,8,64]{4,3,2,1,0:T(8,128)(2,1)} fusion(bf16[2,4,32,8,64]{4,3,2,1,0:T(8,128)(2,1)} %reshape.275, s32[1024]{0:T(1024)S(1)} %pad_clamp_fusion), kind=kCustom, calls=%fused_computation.clone | custom fusion | bytes 1572912 | tf_op jit(solution)/shard_map/jit(_take)/gather | solution.py:179
  69.7 3.0 %gather_fusion.1 = bf16[12,2,32,8,64]{4,3,2,1,0:T(8,128)(2,1)} fusion(bf16[2,4,32,8,64]{4,3,2,1,0:T(8,128)(2,1)} %reshape.277, s32[1024]{0:T(1024)S(1)} %pad_clamp_fusion), kind=kCustom, calls=%fused_computation.1.clone | custom fusion | bytes 1572912 | tf_op jit(solution)/shard_map/jit(_take)/gather | solution.py:178
  72.7 2.2 %select_bitcast_fusion.1 = (bf16[2,4,3,32,8,64]{5,4,3,0,2,1:T(8,128)(2,1)S(1)}, bf16[2,4,3,32,8,64]{5,4,3,0,2,1:T(8,128)(2,1)S(1)}) fusion(bf16[4,3,2,32,8,64]{5,4,3,2,1,0:T(8,128)(2,1)} %bitcast.186, pred[4,3]{1,0:T(4,128)(4,1)S(1)} %get-tuple-element.18, bf16[4,3,2,32,8,64]{5,4,3,2,1,0:T(8,128)(2,1)} %bitcast.187), kind=kLoop, calls=%fused_computation.37 | loop fusion | flops 786432 | bytes 3145740 | tf_op jit(solution)/shard_map/jit(_take)/select_n | solution.py:179
  78.9 1.2 multiply_reduce_fusion
  80.0 2.5 %multiply_convert_fusion = (bf16[2,4,8,32,3,32]{3,5,4,2,1,0:T(8,128)(2,1)}, bf16[2,4,8,32,3,32]{3,5,4,2,1,0:T(8,128)(2,1)S(1)}) fusion(f32[2,4,8,32,3,32]{3,5,4,2,1,0:T(8,128)S(1)} %bitcast.170, f32[2,4,8,32]{3,2,1,0:T(8,128)S(1)} %multiply_reduce_fusion, f32[2,4,8,32]{3,2,1,0:T(8,128)S(1)} %fusion.5, f32[2,4,8,32,3,32]{3,5,4,2,1,0:T(8,128)S(1)} %bitcast.162, ...), kind=kLoop, calls=%fused_computation.6 | loop fusion | flops 1572864 | bytes 2387968 | tf_op jit(solution)/shard_map/convert_element_type | solution.py:243
  82.5 1.1 copy-done.3
  84.3 1.0 copy.37
  85.3 1.4 reshape.278
  86.7 3.4 %convolution_convert_fusion.4 = bf16[256,2048]{1,0:T(8,128)(2,1)} fusion(bf16[256,512]{1,0:T(8,128)(2,1)S(1)} %reshape.278, bf16[1,512,2048]{2,1,0:T(8,128)(2,1)} %param.14), kind=kOutput, calls=%fused_computation.15 | convolution fusion | flops 537395200 | bytes 3407872 | tf_op jit(solution)/shard_map/dot_general | solution.py:196
  90.1 2.1 %convolution_convert_fusion = bf16[512,2048]{1,0:T(8,128)(2,1)} fusion(bf16[256,512]{1,0:T(8,128)(2,1)S(1)} %reshape.278, bf16[256,2048]{1,0:T(8,128)(2,1)S(1)} %bitcast.189), kind=kOutput, calls=%fused_computation.9 | convolution fusion | flops 537919488 | bytes 3407872 | tf_op jit(solution)/shard_map/dot_general | solution.py:161
  92.4 0.7 fusion.40
  93.2 1.0 copy.42
  94.2 1.4 reshape.281
  95.5 1.9 slice.23
  97.4 4.5 %collective-permute-start.1 = (bf16[128,2048]{1,0:T(8,128)(2,1)}, bf16[128,2048]{1,0:T(8,128)(2,1)}, u32[]{:S(2)}, u32[]{:S(2)}) collective-permute-start(bf16[128,2048]{1,0:T(8,128)(2,1)} %slice.23), channel_id=1, source_target_pairs={{0,7},{1,6},{2,5},{3,4},{4,3},{5,2},{6,1},{7,0},{8,15},{9,14},{10,... | collective-permute-start | bytes 1572872 | tf_op jit(solution)/shard_map/ppermute | solution.py:296
  101.9 2.1 %fusion.56 = f32[2,4,8,64,96]{3,4,2,1,0:S(1)} fusion(bf16[2,4,8,32,96]{3,4,2,1,0:T(8,128)(2,1)} %bitcast.172, bf16[2,4,32,8,64]{4,3,2,1,0:T(8,128)(2,1)} %reshape.280), kind=kOutput, calls=%fused_computation.62 | convolution fusion | flops 25165824 | bytes 2228224
  104.0 4.8 %fusion.37 = bf16[2,4,32,8,64]{4,1,3,2,0:T(4,128)(2,1)S(1)} fusion(f32[2,4,3,32,8,64]{5,3,2,4,1,0:T(8,128)S(1)} %bitcast.178, s32[4,3]{0,1:T(4,128)S(1)} %copy.31), kind=kOutput, calls=%fused_computation.47 | convolution fusion | flops 19005488 | bytes 1835056 | tf_op jit(solution)/shard_map/qsk,mqsjhd->mkjhd/dot_general | solution.py:260
  108.8 0.9 copy.49
  109.7 2.1 %reshape.283 = bf16[256,512]{1,0:T(8,128)(2,1)} reshape(bf16[2,4,32,8,64]{4,3,2,1,0:T(8,128)(2,1)} %copy.49) | data formatting | bytes 524288 | tf_op jit(solution)/shard_map/reshape | solution.py:263
  111.7 2.1 %fusion.60 = f32[2,4,8,64,96]{3,4,2,1,0:S(1)} fusion(bf16[2,4,8,32,96]{3,4,2,1,0:T(8,128)(2,1)} %bitcast.171, bf16[2,4,32,8,64]{4,3,2,1,0:T(8,128)(2,1)} %reshape.276), kind=kOutput, calls=%fused_computation.66 | convolution fusion | flops 25165824 | bytes 2228224
  113.8 4.8 %fusion.34 = bf16[2,4,32,8,64]{4,1,3,2,0:T(4,128)(2,1)S(1)} fusion(f32[2,4,3,32,8,64]{5,3,2,4,1,0:T(8,128)S(1)} %bitcast.177, s32[4,3]{0,1:T(4,128)S(1)} %copy.31), kind=kOutput, calls=%fused_computation.46 | convolution fusion | flops 19005488 | bytes 1835056 | tf_op jit(solution)/shard_map/qsk,mqsjhd->mkjhd/dot_general | solution.py:256
  118.6 0.9 copy.46
  119.5 2.1 %reshape.282 = bf16[256,512]{1,0:T(8,128)(2,1)} reshape(bf16[2,4,32,8,64]{4,3,2,1,0:T(8,128)(2,1)} %copy.46) | data formatting | bytes 524288 | tf_op jit(solution)/shard_map/reshape | solution.py:259
  121.6 1.8 convolution_convert_fusion.2
  124.4 0.7 copy-done.17
  125.1 1.0 convolution_add_fusion.1
  126.4 0.8 fusion.6
  128.0 0.7 convolution_convert_fusion.1
  128.8 0.7 convolution_convert_fusion.3
  129.5 0.8 copy-done.1
  130.4 54.0 %ring_scatter.1 = (f32[64,512]{1,0:T(8,128)S(1)}, f32[64,512]{1,0:T(8,128)S(1)}, f32[64,512]{1,0:T(8,128)S(1)}, f32[16,2048]{1,0:T(8,128)S(1)}) custom-call(bf16[4,2,4,64,512]{4,3,2,1,0:T(8,128)(2,1)S(1)} %bitcast.154, bf16[4,2,4,64,512]{4,3,2,1,0:T(8,128)(2,1)S(1)} %bitcast.152, bf16[4,2,4,64,512]{4,3,2,1,0:T(8,128)(2,1)S(1)} %bitcast.153, ...), custom_call_target="tpu_custom_call" | custom-call | tf_op jit(solution)/shard_map/ring_scatter/pallas_call | solution.py:129
  184.4 2.1 %add_convert_fusion = bf16[128,2048]{1,0:T(8,128)(2,1)} fusion(bf16[128,2048]{1,0:T(8,128)(2,1)} %collective-permute-done.1, bf16[128,2048]{1,0:T(8,128)(2,1)S(1)} %copy-done.6, bf16[256,2048]{1,0:T(8,128)(2,1)S(1)} %copy-done.11), kind=kLoop, calls=%fused_computation.59 | loop fusion | flops 1572864 | bytes 2097152 | tf_op jit(solution)/shard_map/convert_element_type | solution.py:320
  186.6 1.0 fusion.55
  (68 shorter events, 12.9 us)
Async XLA Ops:
  0.6 64.3 %copy-start = (bf16[1,2048,512]{2,1,0:T(8,128)(2,1)S(1)}, bf16[1,2048,512]{2,1,0:T(8,128)(2,1)}, u32[]{:S(2)}) copy-start(bf16[1,2048,512]{2,1,0:T(8,128)(2,1)} %param.13) | copy-start | bytes 6291460
  0.6 42.0 %collective-permute-start = (bf16[128,2048]{1,0:T(8,128)(2,1)}, bf16[128,2048]{1,0:T(8,128)(2,1)S(1)}, u32[]{:S(2)}, u32[]{:S(2)}) collective-permute-start(bf16[128,2048]{1,0:T(8,128)(2,1)} %param.9), channel_id=1, source_target_pairs={{0,7},{1,6},{2,5},{3,4},{4,3},{5,2},{6,1},{7,0},{8,15},{9,14},{10,... | collective-permute-start | bytes 1572872 | tf_op jit(solution)/shard_map/ppermute | solution.py:296
  8.1 45.7 %collective-permute-start.2 = (bf16[128,2048]{1,0:T(8,128)(2,1)}, bf16[128,2048]{1,0:T(8,128)(2,1)S(1)}, u32[]{:S(2)}, u32[]{:S(2)}) collective-permute-start(bf16[128,2048]{1,0:T(8,128)(2,1)} %param.10), channel_id=1, source_target_pairs={{0,7},{1,6},{2,5},{3,4},{4,3},{5,2},{6,1},{7,0},{8,15},{9,14},{10,... | collective-permute-start | bytes 1572872 | tf_op jit(solution)/shard_map/ppermute | solution.py:296
  11.5 44.5 %copy-start.19 = (bf16[1,512,2048]{2,1,0:T(8,128)(2,1)S(1)}, bf16[1,512,2048]{2,1,0:T(8,128)(2,1)}, u32[]{:S(2)}) copy-start(bf16[1,512,2048]{2,1,0:T(8,128)(2,1)} %param.14) | copy-start | bytes 6291460
  42.6 14.1 %copy-start.7 = (bf16[128,2048]{1,0:T(8,128)(2,1)}, bf16[128,2048]{1,0:T(8,128)(2,1)S(1)}, u32[]{:S(2)}) copy-start(bf16[128,2048]{1,0:T(8,128)(2,1)S(1)} %collective-permute-done) | copy-start | bytes 1572868
  55.0 1.0 copy-start.12
  57.8 1.9 %copy-start.16 = (bf16[1,2048,512]{2,1,0:T(8,128)(2,1)S(1)}, bf16[1,2048,512]{2,1,0:T(8,128)(2,1)}, u32[]{:S(2)}) copy-start(bf16[1,2048,512]{2,1,0:T(8,128)(2,1)} %param.12) | copy-start | bytes 6291460
  75.0 1.2 copy-start.4
  75.3 1.3 copy-start.10
  76.6 1.0 copy-start.9
  82.5 1.1 copy-start.3
  86.7 3.4 %copy-start.13 = (bf16[2,128,2048]{2,1,0:T(8,128)(2,1)S(1)}, bf16[2,128,2048]{2,1,0:T(8,128)(2,1)}, u32[]{:S(2)}) copy-start(bf16[2,128,2048]{2,1,0:T(8,128)(2,1)} %copy-done.12) | copy-start | bytes 3145732
  90.1 2.1 %copy-start.2 = (bf16[2,4,8,32,3,32]{3,5,4,2,1,0:T(8,128)(2,1)S(1)}, bf16[2,4,8,32,3,32]{3,5,4,2,1,0:T(8,128)(2,1)}, u32[]{:S(2)}) copy-start(bf16[2,4,8,32,3,32]{3,5,4,2,1,0:T(8,128)(2,1)} %get-tuple-element.15) | copy-start | bytes 1179652
  90.1 2.3 %copy-start.5 = (bf16[2,4,3,32,8,64]{5,4,3,0,2,1:T(8,128)(2,1)S(1)}, bf16[2,4,3,32,8,64]{5,4,3,0,2,1:T(8,128)(2,1)}, u32[]{:S(2)}) copy-start(bf16[2,4,3,32,8,64]{5,4,3,0,2,1:T(8,128)(2,1)} %copy-done.4) | copy-start | bytes 2359300
  97.4 87.0 %collective-permute-start.1 = (bf16[128,2048]{1,0:T(8,128)(2,1)}, bf16[128,2048]{1,0:T(8,128)(2,1)}, u32[]{:S(2)}, u32[]{:S(2)}) collective-permute-start(bf16[128,2048]{1,0:T(8,128)(2,1)} %slice.23), channel_id=1, source_target_pairs={{0,7},{1,6},{2,5},{3,4},{4,3},{5,2},{6,1},{7,0},{8,15},{9,14},{10,... | collective-permute-start | bytes 1572872 | tf_op jit(solution)/shard_map/ppermute | solution.py:296
  121.6 1.8 copy-start.18
  123.4 1.0 copy-start.15
  123.4 1.7 copy-start.17
  125.1 1.0 copy-start.6
  125.1 1.2 copy-start.8
  125.1 1.3 copy-start.14
  127.9 58.6 %collective-permute-start.3 = (bf16[128,2048]{1,0:T(8,128)(2,1)S(1)}, bf16[128,2048]{1,0:T(8,128)(2,1)S(1)}, u32[]{:S(2)}, u32[]{:S(2)}) collective-permute-start(bf16[128,2048]{1,0:T(8,128)(2,1)S(1)} %slice_bitcast_fusion), channel_id=1, source_target_pairs={{0,7},{1,6},{2,5},{3,4},{4,3},{5,2},{6,1},{7,0},{8,15},{9,14},{10,... | collective-permute-start | bytes 1572872 | tf_op jit(solution)/shard_map/ppermute | solution.py:296
  128.8 1.6 copy-start.1
  130.4 54.0 %copy-start.11 = (bf16[256,2048]{1,0:T(8,128)(2,1)S(1)}, bf16[256,2048]{1,0:T(8,128)(2,1)}, u32[]{:S(2)}) copy-start(bf16[256,2048]{1,0:T(8,128)(2,1)} %convolution_convert_fusion.4) | copy-start | bytes 3145732
  184.4 2.2 %copy-start.20 = (bf16[128,2048]{1,0:T(8,128)(2,1)S(1)}, bf16[128,2048]{1,0:T(8,128)(2,1)}, u32[]{:S(2)}) copy-start(bf16[128,2048]{1,0:T(8,128)(2,1)} %param.10) | copy-start | bytes 1572868

commit v2 on v0

v2 whole, which is shorter than its diff:
```python
import functools
import math

import jax
import jax.numpy as jnp
from jax import lax
from jax.experimental import pallas as pl
from jax.experimental.pallas import tpu as pltpu
from jax.sharding import PartitionSpec as P

HDIM = 64
BLK = 32
SEQ = 128
NORM_EPS = 1e-05
MESH = pl.DeviceIdType.MESH
X_SIZE, Z_SIZE, Y_SIZE = 4, 2, 4
RING_X = (False, True, False, True)
BF16 = jnp.bfloat16
F32 = jnp.float32


def dot_nn(a, b):
    return lax.dot_general(a, b, (((1,), (0,)), ((), ())), preferred_element_type=F32)


def dot_nt(a, b):
    return lax.dot_general(a, b, (((1,), (1,)), ((), ())), preferred_element_type=F32)


def dot_tn(a, b):
    return lax.dot_general(a, b, (((0,), (0,)), ((), ())), preferred_element_type=F32)


def total(*terms):
    acc = terms[0].astype(F32)
    for term in terms[1:]:
        acc = acc + term.astype(F32)
    return acc


def sublayer_kernel(*refs):
    pattern, x_in, g_in, wq_in, wk_in, wv_in, wo_in = refs[:7]
    hidden_out, grad_in, dwq_out, dwk_out, dwv_out, dwo_out = refs[7:13]
    (
        xs, gs, w_in, w_out, norm_t, att_t, qkv, prob, g_att, g_qkv, factor, g_norm,
        own_term, away_term, back_term, own_ret, away_ret, back_ret,
    ) = refs[13:31]
    parts, far, near, far2, near2, last = (refs[31 + 4 * i : 35 + 4 * i] for i in range(6))
    load_sem, pair_send, pair_recv, ring_send, ring_recv = refs[55:60]
    outs = (dwo_out, dwv_out, dwq_out, dwk_out)

    features = xs.shape[1]
    half = w_out.shape[0]
    heads = half // HDIM
    inv_sqrt = 1.0 / math.sqrt(HDIM)

    dp = lax.axis_index("dp")
    pipe = lax.axis_index("pipe")
    slots = lax.axis_size("pipe")
    x_at = dp // (Z_SIZE * Y_SIZE)
    z_at = lax.rem(dp // Y_SIZE, Z_SIZE)
    y_at = lax.rem(dp, Y_SIZE)

    def device(x, z, y):
        return ((x * Z_SIZE + z) * Y_SIZE + y, pipe)

    def x_to(step):
        return device(lax.rem(x_at + step, X_SIZE), z_at, y_at)

    def y_to(step):
        return device(x_at, z_at, lax.rem(y_at + step, Y_SIZE))

    z_mate = device(x_at, 1 - z_at, y_at)
    mirror = (dp, slots - 1 - pipe)

    first, second = pl.ds(0, SEQ), pl.ds(SEQ, SEQ)
    loads = [
        pltpu.make_async_copy(src, dst, load_sem.at[i])
        for i, (src, dst) in enumerate(
            (
                (x_in, xs.at[first]),
                (wq_in, w_in.at[:, pl.ds(0, half)]),
                (wk_in, w_in.at[:, pl.ds(half, half)]),
                (wv_in, w_in.at[:, pl.ds(2 * half, half)]),
                (wo_in, w_out),
                (g_in, gs.at[first]),
            )
        )
    ]
    for load in loads:
        load.start()

    barrier = pltpu.get_barrier_semaphore()
    for target in (mirror, x_to(1), x_to(3), y_to(1), y_to(3), z_mate):
        pl.semaphore_signal(barrier, inc=1, device_id=target, device_id_type=MESH)
    pl.semaphore_wait(barrier, 6)

    started = []

    def send(src, dst, send_sem, recv_sem, target):
        made = pltpu.make_async_remote_copy(
            src_ref=src, dst_ref=dst, send_sem=send_sem, recv_sem=recv_sem, device_id=target, device_id_type=MESH
        )
        made.start()
        started.append(made)
        return made

    def to_mirror(src, dst, slot):
        return send(src, dst, pair_send.at[slot], pair_recv.at[slot], mirror)

    x_move = to_mirror(x_in, xs.at[second], 0)
    g_move = to_mirror(g_in, gs.at[second], 1)

    row = lax.broadcasted_iota(jnp.int32, (SEQ, SEQ), 0)
    col = lax.broadcasted_iota(jnp.int32, (SEQ, SEQ), 1)
    row_block, col_block = row // BLK, col // BLK
    listed = None
    for j in range(pattern.shape[1]):
        entry = jnp.full((SEQ, SEQ), pattern[0, j], jnp.int32)
        for i in range(1, SEQ // BLK):
            entry = jnp.where(row_block == i, pattern[i, j], entry)
        hit = entry == col_block
        listed = hit if listed is None else jnp.logical_or(listed, hit)
    visible = jnp.logical_and(listed, jnp.logical_or(col_block != row_block, col <= row))
    mask = jnp.where(visible, 1.0, 0.0).astype(F32)

    def head(ref, rows, base, h):
        return ref[rows, base + h * HDIM : base + (h + 1) * HDIM]

    def forward(s):
        rows = slice(s * SEQ, (s + 1) * SEQ)

        def normalise(i, carry):
            at = pl.multiple_of(s * SEQ + i * 16, 16)
            chunk = xs[pl.ds(at, 16), :].astype(F32)
            scale = lax.rsqrt(jnp.mean(chunk * chunk, axis=-1, keepdims=True) + NORM_EPS)
            factor[pl.ds(at, 16), :] = jnp.broadcast_to(scale, (16, 128))
            own_norm[pl.ds(pl.multiple_of(i * 16, 16), 16), :] = (chunk * scale).astype(BF16)
            return carry

        own_norm = own_ret if s == 0 else away_ret
        lax.fori_loop(0, SEQ // 16, normalise, 0)
        for c in range(3):
            cols = slice(c * half, (c + 1) * half)
            qkv[rows, cols] = dot_nn(own_norm[...], w_in[:, cols]).astype(BF16)
        wide = min(512, features)
        for c in range(features // wide):
            norm_t[c * wide : (c + 1) * wide, rows] = own_norm[:, c * wide : (c + 1) * wide].T
        for h in range(0, heads, 2):
            pair = []
            for hh in (h, h + 1):
                score = dot_nt(head(qkv, rows, 0, hh), head(qkv, rows, half, hh)) * inv_sqrt
                expo = jnp.where(mask > 0.5, jnp.exp(score), 0.0)
                p = expo / jnp.sum(expo, axis=-1, keepdims=True)
                prob[s * heads + hh] = p
                pair.append(dot_nn(p.astype(BF16), head(qkv, rows, 2 * half, hh)).astype(BF16))
            both = jnp.concatenate(pair, axis=1)
            g_att[rows, h * HDIM : (h + 2) * HDIM] = both
        att_t[:, rows] = g_att[rows, :].T
        term = own_term if s == 0 else away_term
        for c in range(features // wide):
            cols = slice(c * wide, (c + 1) * wide)
            term[:, cols] = dot_nn(g_att[rows, :], w_out[:, cols]).astype(BF16)

    def backward_heads(s):
        rows = slice(s * SEQ, (s + 1) * SEQ)
        g_att[rows, :] = dot_nt(gs[rows, :], w_out[...]).astype(BF16)
        for h in range(0, heads, 2):
            g_q, g_k, g_v = [], [], []
            for hh in (h, h + 1):
                p = prob[s * heads + hh]
                ga = head(g_att, rows, 0, hh)
                g_prob = dot_nt(ga, head(qkv, rows, 2 * half, hh))
                inner = jnp.sum(p * g_prob, axis=-1, keepdims=True)
                g_score = (p * (g_prob - inner) * inv_sqrt).astype(BF16)
                g_q.append(dot_nn(g_score, head(qkv, rows, half, hh)).astype(BF16))
                g_k.append(dot_tn(g_score, head(qkv, rows, 0, hh)).astype(BF16))
                g_v.append(dot_tn(p.astype(BF16), ga).astype(BF16))
            for c, pieces in enumerate((g_q, g_k, g_v)):
                base = c * half + h * HDIM
                g_qkv[rows, base : base + 2 * HDIM] = jnp.concatenate(pieces, axis=1)

    def backward_input(s):
        rows = slice(s * SEQ, (s + 1) * SEQ)
        wide = min(512, features)
        for c in range(features // wide):
            cols = slice(c * wide, (c + 1) * wide)
            g_norm[:, cols] = dot_nt(g_qkv[rows, :], w_in[cols, :])
        result = own_ret if s == 0 else away_ret

        def returned(i, carry):
            at = pl.multiple_of(i * 16, 16)
            all_at = pl.multiple_of(s * SEQ + i * 16, 16)
            value = xs[pl.ds(all_at, 16), :].astype(F32)
            grad = g_norm[pl.ds(at, 16), :]
            r = factor[pl.ds(all_at, 16), 0:1]
            mean_term = jnp.mean(value * grad, axis=-1, keepdims=True)
            result[pl.ds(at, 16), :] = (r * grad - value * (r * r * r * mean_term)).astype(BF16)
            return carry

        lax.fori_loop(0, SEQ // 16, returned, 0)

    def copy(src, dst, t, slot, target):
        return send(src, dst, ring_send.at[t, slot], ring_recv.at[t, slot], target)

    def part_piece(t, at, z):
        return parts[t].at[at, z] if RING_X[t] else parts[t].at[:, z, at]

    def sum_piece(t, at, z):
        return near[t].at[0, z, at]

    def ring_to(t, stage, step):
        return x_to(step) if RING_X[t] == (stage == 0) else y_to(step)

    def ring_at(t, stage):
        return x_at if RING_X[t] == (stage == 0) else y_at

    msgs = {}

    def ring_start(t, stage):
        piece = (part_piece, sum_piece)[stage]
        far_buf, near_buf = ((far, near), (far2, near2))[stage]
        at, base = ring_at(t, stage), 6 * stage
        opposite, right, left = (lax.rem(at + step, 4) for step in (2, 1, 3))
        msgs[t, base] = copy(piece(t, opposite, 0), far_buf[t].at[0], t, base, ring_to(t, stage, 1))
        msgs[t, base + 1] = copy(piece(t, opposite, 1), far_buf[t].at[1], t, base + 1, ring_to(t, stage, 3))
        msgs[t, base + 2] = copy(piece(t, right, 1), near_buf[t].at[0, 1], t, base + 2, ring_to(t, stage, 1))
        msgs[t, base + 3] = copy(piece(t, left, 0), near_buf[t].at[1, 0], t, base + 3, ring_to(t, stage, 3))

    def ring_forward(t, stage):
        piece = (part_piece, sum_piece)[stage]
        far_buf, near_buf = ((far, near), (far2, near2))[stage]
        at, base = ring_at(t, stage), 6 * stage
        for side, step in ((0, 1), (1, 3)):
            msgs[t, base + side].wait_recv()
            own = piece(t, lax.rem(at + step, 4), side)[...]
            far_buf[t][side] = total(own, far_buf[t][side]).astype(BF16)
            msgs[t, base + 4 + side] = copy(
                far_buf[t].at[side], near_buf[t].at[side, side], t, base + 4 + side, ring_to(t, stage, step)
            )

    def ring_finish(t, stage):
        piece = (part_piece, sum_piece)[stage]
        near_buf = (near, near2)[stage]
        at, base = ring_at(t, stage), 6 * stage
        for slot in range(2, 6):
            msgs[t, base + slot].wait_recv()
        for z in range(2):
            own = piece(t, at, z)[...]
            near_buf[t][0, z] = total(own, near_buf[t][0, z], near_buf[t][1, z]).astype(BF16)

    def weight_grad(t, lhs, rhs):
        block = lhs.shape[0] // X_SIZE
        for i in range(X_SIZE):
            value = dot_nn(lhs[i * block : (i + 1) * block, :], rhs()).astype(BF16)
            parts[t][i] = value.reshape(parts[t].shape[1:])

    def grad_cols(c):
        return lambda: g_qkv[:, c * half : (c + 1) * half]

    for load in loads[:4]:
        load.wait()
    forward_ready = loads[4]
    forward_ready.wait()
    forward(0)
    loads[5].wait()
    backward_heads(0)
    backward_input(0)

    x_move.wait_recv()
    forward(1)
    term_move = to_mirror(away_term, back_term, 2)
    g_move.wait_recv()
    weight_grad(0, att_t, lambda: gs[...])
    ring_start(0, 0)
    backward_heads(1)
    weight_grad(1, norm_t, grad_cols(2))
    ring_start(1, 0)
    weight_grad(2, norm_t, grad_cols(0))
    ring_start(2, 0)
    weight_grad(3, norm_t, grad_cols(1))
    ring_start(3, 0)
    ring_forward(0, 0)
    backward_input(1)
    ret_move = to_mirror(away_ret, back_ret, 3)
    for t in (1, 2, 3):
        ring_forward(t, 0)
    for t in range(4):
        ring_finish(t, 0)
        ring_start(t, 1)
    for t in range(4):
        ring_forward(t, 1)

    def add_up(out, base, one, two):
        def body(i, carry):
            at = pl.ds(pl.multiple_of(i * 16, 16), 16)
            out[at, :] = total(base[at, :], one[at, :], two[at, :]).astype(BF16)
            return carry

        lax.fori_loop(0, SEQ // 16, body, 0)

    term_move.wait_recv()
    add_up(hidden_out, xs, own_term, back_term)
    finals = []
    for t in range(4):
        ring_finish(t, 1)
        finals.append(copy(near2[t].at[0, 1 - z_at], last[t], t, 12, z_mate))
    ret_move.wait_recv()
    add_up(grad_in, gs, own_ret, back_ret)
    for t in range(4):
        finals[t].wait_recv()
        outs[t][...] = total(near2[t][0, z_at], last[t][...])
    for made in started:
        made.wait_send()


def on_device(hidden_in, grad_out, w_query, w_key, w_value, w_out, pattern):
    features, half = w_query.shape[1], w_query.shape[2]
    heads = half // HDIM
    vmem = pl.BlockSpec(memory_space=pltpu.VMEM)
    anywhere = pl.BlockSpec(memory_space=pl.ANY)
    ranks = X_SIZE * Z_SIZE * Y_SIZE
    tails = [(half // ranks, features)] + [(features // ranks, half)] * 3
    both, one = (2 * SEQ, features), (SEQ, features)
    scratch = [
        pltpu.VMEM(both, BF16),
        pltpu.VMEM(both, BF16),
        pltpu.VMEM((features, 3 * half), BF16),
        pltpu.VMEM((half, features), BF16),
        pltpu.VMEM((features, 2 * SEQ), BF16),
        pltpu.VMEM((half, 2 * SEQ), BF16),
        pltpu.VMEM((2 * SEQ, 3 * half), BF16),
        pltpu.VMEM((2 * heads, SEQ, SEQ), F32),
        pltpu.VMEM((2 * SEQ, half), BF16),
        pltpu.VMEM((2 * SEQ, 3 * half), BF16),
        pltpu.VMEM((2 * SEQ, 128), F32),
        pltpu.VMEM(one, F32),
    ] + [pltpu.VMEM(one, BF16)] * 6
    for lead in ((X_SIZE, Z_SIZE, Y_SIZE), (2, 4), (2, 2, 4), (2,), (2, 2), ()):
        scratch += [pltpu.VMEM(lead + tail, BF16) for tail in tails]
    scratch += [
        pltpu.SemaphoreType.DMA((6,)),
        pltpu.SemaphoreType.DMA((4,)),
        pltpu.SemaphoreType.DMA((4,)),
        pltpu.SemaphoreType.DMA((4, 13)),
        pltpu.SemaphoreType.DMA((4, 13)),
    ]
    outs = pl.pallas_call(
        sublayer_kernel,
        out_shape=(jax.ShapeDtypeStruct(one, BF16),) * 2
        + tuple(jax.ShapeDtypeStruct(tail, F32) for tail in tails[1:] + tails[:1]),
        in_specs=[pl.BlockSpec(memory_space=pltpu.SMEM)] + [anywhere] * 6,
        out_specs=(vmem,) * 6,
        scratch_shapes=scratch,
        compiler_params=pltpu.CompilerParams(
            collective_id=0, has_side_effects=True, vmem_limit_bytes=56 * 1024 * 1024
        ),
        name="sublayer",
    )(pattern, hidden_in, grad_out, w_query[0], w_key[0], w_value[0], w_out[0])
    return (outs[0], outs[1]) + tuple(out[None] for out in outs[2:])


def solution(mesh):
    in_specs = (
        P(("dp", "pipe"), None),
        P(("dp", "pipe"), None),
        P("pipe", None, None),
        P("pipe", None, None),
        P("pipe", None, None),
        P("pipe", None, None),
        P(),
    )
    out_specs = (
        P(("dp", "pipe"), None),
        P(("dp", "pipe"), None),
        P("pipe", "dp", None),
        P("pipe", "dp", None),
        P("pipe", "dp", None),
        P("pipe", "dp", None),
    )
    return jax.shard_map(
        on_device, mesh=mesh, in_specs=in_specs, out_specs=out_specs, check_vma=False
    )
```

time: 891 us -> 134 us (0.15)
  the two profiles are of different devices: /device:TPU:64 before, /device:TPU:1 now
where the time goes in v2:
time: 134 us
  Pallas kernels  127 us (95%)
  local copies, waits for them, and re-layouts  6.46 us (5%)
    pallas_call x1, Pallas kernels, on_device(): pl.pallas_call(sublayer_kernel, out_shape=(jax.ShapeDtypeStruct(one, BF16...  127 us
    unnamed x14, local copies, waits for them, and re-layouts  6.46 us

profile of v2, /device:TPU:1, one launch (start us, length us, event | category | flops | bytes accessed | tf_op | source)
XLA Modules:
  0.0 134.2 jit_solution(17628722809187774205)
XLA Ops:
  0.6 127.0 %sublayer.1 = (bf16[128,2048]{1,0:T(8,128)(2,1)}, bf16[128,2048]{1,0:T(8,128)(2,1)}, f32[64,512]{1,0:T(8,128)}, f32[64,512]{1,0:T(8,128)}, f32[64,512]{1,0:T(8,128)}, /*index=5*/f32[16,2048]{1,0:T(8,128)}) custom-call(s32[4,3]{1,0:T(4,128)} %refs_0_.1, bf16[128,2048]{1,0:T(8,128)(2,1)} %refs_1_.1, bf16[128,2048]{1,0:T(8,128)(2,1)} %refs_2_.1, ...), custom_call_target="tpu_custom_call" | custom-call | tf_op jit(solution)/shard_map/sublayer/pallas_call | solution.py:348
  127.7 0.0 copy-start.3
  127.7 0.0 copy-start.2
  127.7 0.0 copy-start.1
  127.7 0.0 copy-start
  127.7 1.9 %copy.19 = bf16[128,2048]{1,0:T(8,128)(2,1)} copy(bf16[128,2048]{1,0:T(8,128)(2,1)} %get-tuple-element.24) | data formatting | bytes 1048576
  129.7 1.9 %copy.20 = bf16[128,2048]{1,0:T(8,128)(2,1)} copy(bf16[128,2048]{1,0:T(8,128)(2,1)} %get-tuple-element.25) | data formatting | bytes 1048576
  131.5 0.0 copy-done.3
  131.5 0.7 copy.21
  132.2 0.0 copy-done.2
  132.2 0.7 copy.22
  132.9 0.0 copy-done.1
  132.9 0.7 copy.23
  133.5 0.0 copy-done
  133.5 0.7 copy.24
Async XLA Ops:
  127.7 3.9 %copy-start.3 = (f32[64,512]{1,0:T(8,128)S(1)}, f32[64,512]{1,0:T(8,128)}, u32[]{:S(2)}) copy-start(f32[64,512]{1,0:T(8,128)} %get-tuple-element.14) | copy-start | bytes 393220
  127.7 4.5 %copy-start.2 = (f32[64,512]{1,0:T(8,128)S(1)}, f32[64,512]{1,0:T(8,128)}, u32[]{:S(2)}) copy-start(f32[64,512]{1,0:T(8,128)} %get-tuple-element.15) | copy-start | bytes 393220
  127.7 5.2 %copy-start.1 = (f32[64,512]{1,0:T(8,128)S(1)}, f32[64,512]{1,0:T(8,128)}, u32[]{:S(2)}) copy-start(f32[64,512]{1,0:T(8,128)} %get-tuple-element.16) | copy-start | bytes 393220
  127.7 5.8 %copy-start = (f32[16,2048]{1,0:T(8,128)S(1)}, f32[16,2048]{1,0:T(8,128)}, u32[]{:S(2)}) copy-start(f32[16,2048]{1,0:T(8,128)} %get-tuple-element.17) | copy-start | bytes 393220

commit v3 on v2

--- a/solution.py
+++ b/solution.py
@@ -14,7 +14,8 @@
 NORM_EPS = 1e-05
 MESH = pl.DeviceIdType.MESH
 X_SIZE, Z_SIZE, Y_SIZE = 4, 2, 4
-RING_X = (False, True, False, True)
+RING_X = (False, True, True, True)
+STEPS = (1, 3, 2)
 BF16 = jnp.bfloat16
 F32 = jnp.float32
 
@@ -44,15 +45,17 @@
     (
         xs, gs, w_in, w_out, norm_t, att_t, qkv, prob, g_att, g_qkv, factor, g_norm,
         own_term, away_term, back_term, own_ret, away_ret, back_ret,
-    ) = refs[13:31]
-    parts, far, near, far2, near2, last = (refs[31 + 4 * i : 35 + 4 * i] for i in range(6))
-    load_sem, pair_send, pair_recv, ring_send, ring_recv = refs[55:60]
+        norm_y, grad_y, att_x, g_x, out_sum, out_recv,
+    ) = refs[13:37]
+    parts, far, near, last = (refs[37 + 4 * i : 41 + 4 * i] for i in range(4))
+    load_sem, pair_send, pair_recv, ring_send, ring_recv, gather_send, gather_recv = refs[53:60]
     outs = (dwo_out, dwv_out, dwq_out, dwk_out)
 
     features = xs.shape[1]
     half = w_out.shape[0]
     heads = half // HDIM
     inv_sqrt = 1.0 / math.sqrt(HDIM)
+    quarter = features // 4
 
     dp = lax.axis_index("dp")
     pipe = lax.axis_index("pipe")
@@ -91,9 +94,9 @@
         load.start()
 
     barrier = pltpu.get_barrier_semaphore()
-    for target in (mirror, x_to(1), x_to(3), y_to(1), y_to(3), z_mate):
+    for target in (mirror, z_mate) + tuple(to(step) for to in (x_to, y_to) for step in STEPS):
         pl.semaphore_signal(barrier, inc=1, device_id=target, device_id_type=MESH)
-    pl.semaphore_wait(barrier, 6)
+    pl.semaphore_wait(barrier, 8)
 
     started = []
 
@@ -110,6 +113,44 @@
 
     x_move = to_mirror(x_in, xs.at[second], 0)
     g_move = to_mirror(g_in, gs.at[second], 1)
+
+    gathers = {}
+
+    def gather(kind, src_of, dst_of, to):
+        gathers[kind] = [
+            send(src_of(step), dst_of(3 - step), gather_send.at[kind, i], gather_recv.at[kind, i], to(step))
+            for i, step in enumerate(STEPS)
+        ]
+
+    def arrived(*kinds):
+        for kind in kinds:
+            for move in gathers[kind]:
+                move.wait_recv()
+
+    def seq(s):
+        return pl.ds(s * SEQ, SEQ)
+
+    def gather_norm(s):
+        gather(
+            s,
+            lambda step: norm_t.at[:, lax.rem(y_at + step, 4), :, seq(s)],
+            lambda i: norm_y.at[i, :, :, seq(s)],
+            y_to,
+        )
+
+    def gather_att(s):
+        gather(2 + s, lambda step: att_t.at[:, seq(s)], lambda i: att_x.at[i, :, seq(s)], x_to)
+
+    def gather_out_grad(s):
+        def piece(step):
+            column = pl.multiple_of(lax.rem(x_at + step, 4) * quarter, quarter)
+            return gs.at[seq(s), pl.ds(column, quarter)]
+
+        gather(4 + s, piece, lambda i: g_x.at[i, seq(s), :], x_to)
+
+    def gather_grad(s, c):
+        cols = pl.ds(c * half, half)
+        gather(6 + 3 * s + c, lambda step: g_qkv.at[seq(s), cols], lambda i: grad_y.at[i, seq(s), cols], y_to)
 
     row = lax.broadcasted_iota(jnp.int32, (SEQ, SEQ), 0)
     col = lax.broadcasted_iota(jnp.int32, (SEQ, SEQ), 1)
@@ -140,12 +181,14 @@
 
         own_norm = own_ret if s == 0 else away_ret
         lax.fori_loop(0, SEQ // 16, normalise, 0)
+        for c in range(4):
+            flipped = own_norm[:, c * quarter : (c + 1) * quarter].T
+            norm_t[2 * c : 2 * c + 2, :, :, rows] = flipped.reshape((2,) + norm_t.shape[1:3] + (SEQ,))
+        gather_norm(s)
         for c in range(3):
             cols = slice(c * half, (c + 1) * half)
             qkv[rows, cols] = dot_nn(own_norm[...], w_in[:, cols]).astype(BF16)
         wide = min(512, features)
-        for c in range(features // wide):
-            norm_t[c * wide : (c + 1) * wide, rows] = own_norm[:, c * wide : (c + 1) * wide].T
         for h in range(0, heads, 2):
             pair = []
             for hh in (h, h + 1):
@@ -157,6 +200,7 @@
             both = jnp.concatenate(pair, axis=1)
             g_att[rows, h * HDIM : (h + 2) * HDIM] = both
         att_t[:, rows] = g_att[rows, :].T
+        gather_att(s)
         term = own_term if s == 0 else away_term
         for c in range(features // wide):
             cols = slice(c * wide, (c + 1) * wide)
@@ -179,6 +223,8 @@
             for c, pieces in enumerate((g_q, g_k, g_v)):
                 base = c * half + h * HDIM
                 g_qkv[rows, base : base + 2 * HDIM] = jnp.concatenate(pieces, axis=1)
+        for c in (2, 0, 1):
+            gather_grad(s, c)
 
     def backward_input(s):
         rows = slice(s * SEQ, (s + 1) * SEQ)
@@ -200,70 +246,65 @@
 
         lax.fori_loop(0, SEQ // 16, returned, 0)
 
+    msgs = {}
+
+    def piece(t, at, z):
+        return parts[t].at[at, z] if RING_X[t] else parts[t].at[:, z, at]
+
+    def ring_to(t, step):
+        return x_to(step) if RING_X[t] else y_to(step)
+
     def copy(src, dst, t, slot, target):
-        return send(src, dst, ring_send.at[t, slot], ring_recv.at[t, slot], target)
-
-    def part_piece(t, at, z):
-        return parts[t].at[at, z] if RING_X[t] else parts[t].at[:, z, at]
-
-    def sum_piece(t, at, z):
-        return near[t].at[0, z, at]
-
-    def ring_to(t, stage, step):
-        return x_to(step) if RING_X[t] == (stage == 0) else y_to(step)
-
-    def ring_at(t, stage):
-        return x_at if RING_X[t] == (stage == 0) else y_at
-
-    msgs = {}
-
-    def ring_start(t, stage):
-        piece = (part_piece, sum_piece)[stage]
-        far_buf, near_buf = ((far, near), (far2, near2))[stage]
-        at, base = ring_at(t, stage), 6 * stage
+        msgs[t, slot] = send(src, dst, ring_send.at[t, slot], ring_recv.at[t, slot], target)
+
+    def ring_start(t):
+        at = x_at if RING_X[t] else y_at
         opposite, right, left = (lax.rem(at + step, 4) for step in (2, 1, 3))
-        msgs[t, base] = copy(piece(t, opposite, 0), far_buf[t].at[0], t, base, ring_to(t, stage, 1))
-        msgs[t, base + 1] = copy(piece(t, opposite, 1), far_buf[t].at[1], t, base + 1, ring_to(t, stage, 3))
-        msgs[t, base + 2] = copy(piece(t, right, 1), near_buf[t].at[0, 1], t, base + 2, ring_to(t, stage, 1))
-        msgs[t, base + 3] = copy(piece(t, left, 0), near_buf[t].at[1, 0], t, base + 3, ring_to(t, stage, 3))
-
-    def ring_forward(t, stage):
-        piece = (part_piece, sum_piece)[stage]
-        far_buf, near_buf = ((far, near), (far2, near2))[stage]
-        at, base = ring_at(t, stage), 6 * stage
+        copy(piece(t, opposite, 0), far[t].at[0], t, 0, ring_to(t, 1))
+        copy(piece(t, opposite, 1), far[t].at[1], t, 1, ring_to(t, 3))
+        copy(piece(t, right, 1), near[t].at[0, 1], t, 2, ring_to(t, 1))
+        copy(piece(t, left, 0), near[t].at[1, 0], t, 3, ring_to(t, 3))
+
+    def ring_forward(t):
+        at = x_at if RING_X[t] else y_at
         for side, step in ((0, 1), (1, 3)):
-            msgs[t, base + side].wait_recv()
+            msgs[t, side].wait_recv()
             own = piece(t, lax.rem(at + step, 4), side)[...]
-            far_buf[t][side] = total(own, far_buf[t][side]).astype(BF16)
-            msgs[t, base + 4 + side] = copy(
-                far_buf[t].at[side], near_buf[t].at[side, side], t, base + 4 + side, ring_to(t, stage, step)
-            )
-
-    def ring_finish(t, stage):
-        piece = (part_piece, sum_piece)[stage]
-        near_buf = (near, near2)[stage]
-        at, base = ring_at(t, stage), 6 * stage
+            far[t][side] = total(own, far[t][side]).astype(BF16)
+            copy(far[t].at[side], near[t].at[side, side], t, 4 + side, ring_to(t, step))
+
+    def ring_finish(t):
+        at = x_at if RING_X[t] else y_at
         for slot in range(2, 6):
-            msgs[t, base + slot].wait_recv()
+            msgs[t, slot].wait_recv()
         for z in range(2):
             own = piece(t, at, z)[...]
-            near_buf[t][0, z] = total(own, near_buf[t][0, z], near_buf[t][1, z]).astype(BF16)
-
-    def weight_grad(t, lhs, rhs):
-        block = lhs.shape[0] // X_SIZE
+            near[t][0, z] = total(own, near[t][0, z], near[t][1, z]).astype(BF16)
+        copy(near[t].at[0, 1 - z_at], last[t], t, 6, z_mate)
+
+    def weight_grad(t, c):
+        cols = slice(c * half, (c + 1) * half)
         for i in range(X_SIZE):
-            value = dot_nn(lhs[i * block : (i + 1) * block, :], rhs()).astype(BF16)
-            parts[t][i] = value.reshape(parts[t].shape[1:])
-
-    def grad_cols(c):
-        return lambda: g_qkv[:, c * half : (c + 1) * half]
-
-    for load in loads[:4]:
+            tall = (quarter // 4, 2 * SEQ)
+            acc = dot_nn(norm_t[2 * i : 2 * i + 2, y_at].reshape(tall), g_qkv[:, cols])
+            for j in range(3):
+                acc = acc + dot_nn(norm_y[j, 2 * i : 2 * i + 2].reshape(tall), grad_y[j, :, cols])
+            parts[t][i] = acc.astype(BF16).reshape(parts[t].shape[1:])
+
+    def out_weight_grad():
+        block = half // X_SIZE
+        mine = gs[:, pl.ds(pl.multiple_of(x_at * quarter, quarter), quarter)]
+        for i in range(X_SIZE):
+            rows = slice(i * block, (i + 1) * block)
+            acc = dot_nn(att_t[rows, :], mine)
+            for j in range(3):
+                acc = acc + dot_nn(att_x[j, rows, :], g_x[j])
+            parts[0][i] = acc.astype(BF16).reshape(parts[0].shape[1:])
+
+    for load in loads:
         load.wait()
-    forward_ready = loads[4]
-    forward_ready.wait()
+    gather_out_grad(0)
     forward(0)
-    loads[5].wait()
     backward_heads(0)
     backward_input(0)
 
@@ -271,25 +312,34 @@
     forward(1)
     term_move = to_mirror(away_term, back_term, 2)
     g_move.wait_recv()
-    weight_grad(0, att_t, lambda: gs[...])
-    ring_start(0, 0)
+    gather_out_grad(1)
     backward_heads(1)
-    weight_grad(1, norm_t, grad_cols(2))
-    ring_start(1, 0)
-    weight_grad(2, norm_t, grad_cols(0))
-    ring_start(2, 0)
-    weight_grad(3, norm_t, grad_cols(1))
-    ring_start(3, 0)
-    ring_forward(0, 0)
     backward_input(1)
     ret_move = to_mirror(away_ret, back_ret, 3)
-    for t in (1, 2, 3):
-        ring_forward(t, 0)
-    for t in range(4):
-        ring_finish(t, 0)
-        ring_start(t, 1)
-    for t in range(4):
-        ring_forward(t, 1)
+    arrived(2, 3, 4, 5)
+    out_weight_grad()
+    ring_start(0)
+    arrived(0, 1, 8, 11)
+    weight_grad(1, 2)
+    ring_start(1)
+    ring_forward(0)
+    arrived(6, 9)
+    weight_grad(2, 0)
+    ring_start(2)
+    ring_forward(1)
+    arrived(7, 10)
+    weight_grad(3, 1)
+    ring_start(3)
+    ring_finish(0)
+    ring_forward(2)
+    ring_finish(1)
+    ring_forward(3)
+    msgs[0, 6].wait_recv()
+    out_sum[...] = total(near[0][0, z_at], last[0][...])
+    spread = [
+        send(out_sum.at[lax.rem(x_at + step, 4)], out_recv.at[3 - step], ring_send.at[0, 7 + i], ring_recv.at[0, 7 + i], x_to(step))
+        for i, step in enumerate(STEPS)
+    ]
 
     def add_up(out, base, one, two):
         def body(i, carry):
@@ -301,15 +351,22 @@
 
     term_move.wait_recv()
     add_up(hidden_out, xs, own_term, back_term)
-    finals = []
-    for t in range(4):
-        ring_finish(t, 1)
-        finals.append(copy(near2[t].at[0, 1 - z_at], last[t], t, 12, z_mate))
+    ring_finish(2)
+    ring_finish(3)
     ret_move.wait_recv()
     add_up(grad_in, gs, own_ret, back_ret)
-    for t in range(4):
-        finals[t].wait_recv()
-        outs[t][...] = total(near2[t][0, z_at], last[t][...])
+    for i, step in enumerate(STEPS):
+        spread[i].wait_recv()
+
+    def out_columns(at):
+        return pl.ds(pl.multiple_of(at * quarter, quarter), quarter)
+
+    dwo_out[:, out_columns(x_at)] = out_sum[x_at]
+    for r in (1, 2, 3):
+        dwo_out[:, out_columns(lax.rem(x_at + r, 4))] = out_recv[r - 1]
+    for t in (1, 2, 3):
+        msgs[t, 6].wait_recv()
+        outs[t][...] = total(near[t][0, z_at], last[t][...])
     for made in started:
         made.wait_send()
 
@@ -327,7 +384,7 @@
         pltpu.VMEM(both, BF16),
         pltpu.VMEM((features, 3 * half), BF16),
         pltpu.VMEM((half, features), BF16),
-        pltpu.VMEM((features, 2 * SEQ), BF16),
+        pltpu.VMEM((8, 4, features // ranks, 2 * SEQ), BF16),
         pltpu.VMEM((half, 2 * SEQ), BF16),
         pltpu.VMEM((2 * SEQ, 3 * half), BF16),
         pltpu.VMEM((2 * heads, SEQ, SEQ), F32),
@@ -336,14 +393,27 @@
         pltpu.VMEM((2 * SEQ, 128), F32),
         pltpu.VMEM(one, F32),
     ] + [pltpu.VMEM(one, BF16)] * 6
-    for lead in ((X_SIZE, Z_SIZE, Y_SIZE), (2, 4), (2, 2, 4), (2,), (2, 2), ()):
-        scratch += [pltpu.VMEM(lead + tail, BF16) for tail in tails]
+    quarter = features // 4
+    small = (half // ranks, quarter)
+    scratch += [
+        pltpu.VMEM((3, 8, features // ranks, 2 * SEQ), BF16),
+        pltpu.VMEM((3, 2 * SEQ, 3 * half), BF16),
+        pltpu.VMEM((3, half, 2 * SEQ), BF16),
+        pltpu.VMEM((3, 2 * SEQ, quarter), BF16),
+        pltpu.VMEM((4,) + small, F32),
+        pltpu.VMEM((3,) + small, F32),
+        pltpu.VMEM((X_SIZE, Z_SIZE, Y_SIZE) + small, BF16),
+    ] + [pltpu.VMEM((X_SIZE, Z_SIZE) + tails[1], BF16)] * 3
+    for lead in ((2,), (2, 2), ()):
+        scratch += [pltpu.VMEM(lead + tail, BF16) for tail in [(4,) + small] + tails[1:]]
     scratch += [
         pltpu.SemaphoreType.DMA((6,)),
         pltpu.SemaphoreType.DMA((4,)),
         pltpu.SemaphoreType.DMA((4,)),
-        pltpu.SemaphoreType.DMA((4, 13)),
-        pltpu.SemaphoreType.DMA((4, 13)),
+        pltpu.SemaphoreType.DMA((4, 10)),
+        pltpu.SemaphoreType.DMA((4, 10)),
+        pltpu.SemaphoreType.DMA((12, 3)),
+        pltpu.SemaphoreType.DMA((12, 3)),
     ]
     outs = pl.pallas_call(
         sublayer_kernel,

time: 134 us -> 120 us (0.90)
  Pallas kernels: 127 us -> 113 us
    pallas_call x1, Pallas kernels: 127 us -> 113 us  [on_device(): pl.pallas_call(sublayer_kernel, out_shape=(jax.ShapeDtypeStruct(one, BF16...]
where the time goes in v3:
time: 120 us
  Pallas kernels  113 us (94%)
  local copies, waits for them, and re-layouts  6.46 us (5%)
    pallas_call x1, Pallas kernels, on_device(): pl.pallas_call(sublayer_kernel, out_shape=(jax.ShapeDtypeStruct(one, BF16...  113 us
    unnamed x14, local copies, waits for them, and re-layouts  6.46 us

profile of v3, /device:TPU:1, one launch (start us, length us, event | category | flops | bytes accessed | tf_op | source)
XLA Modules:
  0.0 120.0 jit_solution(1628133644693790424)
XLA Ops:
  0.6 112.9 %sublayer.1 = (bf16[128,2048]{1,0:T(8,128)(2,1)}, bf16[128,2048]{1,0:T(8,128)(2,1)}, f32[64,512]{1,0:T(8,128)}, f32[64,512]{1,0:T(8,128)}, f32[64,512]{1,0:T(8,128)}, /*index=5*/f32[16,2048]{1,0:T(8,128)}) custom-call(s32[4,3]{1,0:T(4,128)} %refs_0_.1, bf16[128,2048]{1,0:T(8,128)(2,1)} %refs_1_.1, bf16[128,2048]{1,0:T(8,128)(2,1)} %refs_2_.1, ...), custom_call_target="tpu_custom_call" | custom-call | tf_op jit(solution)/shard_map/sublayer/pallas_call | solution.py:418
  113.5 0.0 copy-start.3
  113.5 0.0 copy-start.2
  113.5 0.0 copy-start.1
  113.5 0.0 copy-start
  113.5 1.9 %copy.19 = bf16[128,2048]{1,0:T(8,128)(2,1)} copy(bf16[128,2048]{1,0:T(8,128)(2,1)} %get-tuple-element.24) | data formatting | bytes 1048576
  115.5 1.9 %copy.20 = bf16[128,2048]{1,0:T(8,128)(2,1)} copy(bf16[128,2048]{1,0:T(8,128)(2,1)} %get-tuple-element.25) | data formatting | bytes 1048576
  117.4 0.0 copy-done.3
  117.4 0.7 copy.21
  118.0 0.0 copy-done.2
  118.0 0.7 copy.22
  118.7 0.0 copy-done.1
  118.7 0.7 copy.23
  119.3 0.0 copy-done
  119.3 0.7 copy.24
Async XLA Ops:
  113.5 3.9 %copy-start.3 = (f32[64,512]{1,0:T(8,128)S(1)}, f32[64,512]{1,0:T(8,128)}, u32[]{:S(2)}) copy-start(f32[64,512]{1,0:T(8,128)} %get-tuple-element.14) | copy-start | bytes 393220
  113.5 4.5 %copy-start.2 = (f32[64,512]{1,0:T(8,128)S(1)}, f32[64,512]{1,0:T(8,128)}, u32[]{:S(2)}) copy-start(f32[64,512]{1,0:T(8,128)} %get-tuple-element.15) | copy-start | bytes 393220
  113.5 5.2 %copy-start.1 = (f32[64,512]{1,0:T(8,128)S(1)}, f32[64,512]{1,0:T(8,128)}, u32[]{:S(2)}) copy-start(f32[64,512]{1,0:T(8,128)} %get-tuple-element.16) | copy-start | bytes 393220
  113.5 5.8 %copy-start = (f32[16,2048]{1,0:T(8,128)S(1)}, f32[16,2048]{1,0:T(8,128)}, u32[]{:S(2)}) copy-start(f32[16,2048]{1,0:T(8,128)} %get-tuple-element.17) | copy-start | bytes 393220

commit v4 on v3

--- a/solution.py
+++ b/solution.py
@@ -14,7 +14,7 @@
 NORM_EPS = 1e-05
 MESH = pl.DeviceIdType.MESH
 X_SIZE, Z_SIZE, Y_SIZE = 4, 2, 4
-RING_X = (False, True, True, True)
+RING_X = (False, True, True, True, False)
 STEPS = (1, 3, 2)
 BF16 = jnp.bfloat16
 F32 = jnp.float32
@@ -43,13 +43,14 @@
     pattern, x_in, g_in, wq_in, wk_in, wv_in, wo_in = refs[:7]
     hidden_out, grad_in, dwq_out, dwk_out, dwv_out, dwo_out = refs[7:13]
     (
-        xs, gs, w_in, w_out, norm_t, att_t, qkv, prob, g_att, g_qkv, factor, g_norm,
-        own_term, away_term, back_term, own_ret, away_ret, back_ret,
-        norm_y, grad_y, att_x, g_x, out_sum, out_recv,
-    ) = refs[13:37]
-    parts, far, near, last = (refs[37 + 4 * i : 41 + 4 * i] for i in range(4))
-    load_sem, pair_send, pair_recv, ring_send, ring_recv, gather_send, gather_recv = refs[53:60]
-    outs = (dwo_out, dwv_out, dwq_out, dwk_out)
+        xs, gs, w_in, w_out, w_far, norm_t, att_t, qkv, prob, g_att, g_qkv, factor, g_norm,
+        own_term, far_term, own_ret, away_ret, back_ret, far_grad_out, far_grad_in, far_att,
+        far_own, far_part, far_part_in, term_part,
+        norm_y, grad_y, att_x, g_x, out_sum, out_cast, out_own, out_far, out_back,
+    ) = refs[13:47]
+    parts, far, near, last = (refs[47 + 5 * i : 52 + 5 * i] for i in range(4))
+    load_sem, pair_send, pair_recv, ring_send, ring_recv, gather_send, gather_recv = refs[67:74]
+    outs = (None, dwv_out, dwq_out, dwk_out)
 
     features = xs.shape[1]
     half = w_out.shape[0]
@@ -82,11 +83,11 @@
         for i, (src, dst) in enumerate(
             (
                 (x_in, xs.at[first]),
+                (g_in, gs),
                 (wq_in, w_in.at[:, pl.ds(0, half)]),
                 (wk_in, w_in.at[:, pl.ds(half, half)]),
                 (wv_in, w_in.at[:, pl.ds(2 * half, half)]),
                 (wo_in, w_out),
-                (g_in, gs.at[first]),
             )
         )
     ]
@@ -111,8 +112,14 @@
     def to_mirror(src, dst, slot):
         return send(src, dst, pair_send.at[slot], pair_recv.at[slot], mirror)
 
-    x_move = to_mirror(x_in, xs.at[second], 0)
-    g_move = to_mirror(g_in, gs.at[second], 1)
+    def columns(at):
+        return pl.ds(pl.multiple_of(at * quarter, quarter), quarter)
+
+    share = half // (Z_SIZE * Y_SIZE)
+    share_rows = pl.ds(pl.multiple_of((z_at * Y_SIZE + y_at) * share, share), share)
+    w_move = to_mirror(wo_in.at[share_rows, columns(x_at)], w_far.at[z_at, y_at], 1)
+    head_rows = SEQ // 4
+    x_moves = [to_mirror(x_in.at[pl.ds(0, head_rows), :], xs.at[pl.ds(SEQ, head_rows), :], 0)]
 
     gathers = {}
 
@@ -133,24 +140,74 @@
     def gather_norm(s):
         gather(
             s,
-            lambda step: norm_t.at[:, lax.rem(y_at + step, 4), :, seq(s)],
-            lambda i: norm_y.at[i, :, :, seq(s)],
+            lambda step: norm_t.at[s, lax.rem(y_at + step, 4)],
+            lambda i: norm_y.at[i, s],
             y_to,
         )
 
-    def gather_att(s):
-        gather(2 + s, lambda step: att_t.at[:, seq(s)], lambda i: att_x.at[i, :, seq(s)], x_to)
-
-    def gather_out_grad(s):
+    def gather_att(slot):
+        rows = pl.ds(slot * half, half)
+        gather(2 + slot, lambda step: att_t.at[rows, :], lambda i: att_x.at[i, rows, :], x_to)
+
+    def gather_out_grad():
         def piece(step):
-            column = pl.multiple_of(lax.rem(x_at + step, 4) * quarter, quarter)
-            return gs.at[seq(s), pl.ds(column, quarter)]
-
-        gather(4 + s, piece, lambda i: g_x.at[i, seq(s), :], x_to)
+            return gs.at[:, columns(lax.rem(x_at + step, 4))]
+
+        gather(4, piece, lambda i: g_x.at[i], x_to)
+
+    def grad_move(kind, slot, src, dst, step):
+        return send(src, dst, gather_send.at[kind, slot], gather_recv.at[kind, slot], y_to(step))
 
     def gather_grad(s, c):
-        cols = pl.ds(c * half, half)
-        gather(6 + 3 * s + c, lambda step: g_qkv.at[seq(s), cols], lambda i: grad_y.at[i, seq(s), cols], y_to)
+        kind = 6 + 3 * s + c
+        gathers[kind] = [
+            grad_move(kind, i, g_qkv.at[c, seq(s)], grad_y.at[3 - step, c, seq(s)], step)
+            for i, step in enumerate((1, 3))
+        ]
+
+    def relay_grad(s, c):
+        kind = 6 + 3 * s + c
+        passed = []
+        for i, step in enumerate((1, 3)):
+            gathers[kind][i].wait_recv()
+            rows = pl.ds(s * SEQ + i * (SEQ // 2), SEQ // 2)
+            passed.append(grad_move(kind, 2 + i, grad_y.at[3 - step, c, rows], grad_y.at[1, c, rows], step))
+        gathers[kind] = passed
+
+    def far_pair():
+        w_move.wait_recv()
+        src = w_far.at[z_at, y_at]
+        gathers[13] = [send(src, src, gather_send.at[13, 0], gather_recv.at[13, 0], z_mate)]
+
+    def far_spread():
+        arrived(13)
+        src = w_far.at[:, y_at]
+        gathers[12] = [
+            send(src, src, gather_send.at[12, i], gather_recv.at[12, i], y_to(step)) for i, step in enumerate(STEPS)
+        ]
+
+    def far_grad_parts():
+        arrived(12, 4)
+        far_own[...] = dot_nt(gs[:, columns(x_at)], w_far[...].reshape(half, quarter))
+        gathers[14] = []
+        for i, step in enumerate(STEPS):
+            far_part[step - 1] = dot_nt(g_x[step - 1], w_far[...].reshape(half, quarter)).astype(BF16)
+            src, dst = far_part.at[step - 1], far_part_in.at[3 - step]
+            gathers[14].append(send(src, dst, gather_send.at[14, i], gather_recv.at[14, i], x_to(step)))
+
+    def far_grad_sum():
+        arrived(14)
+        far_grad_out[...] = total(far_own[...], far_part_in[0], far_part_in[1], far_part_in[2]).astype(BF16)
+        return to_mirror(far_grad_out, far_grad_in, 2)
+
+    def far_term_parts():
+        far_term[:, columns(x_at)] = dot_nn(far_att[...], w_far[...].reshape(half, quarter)).astype(BF16)
+        gathers[15] = []
+        for i, step in enumerate(STEPS):
+            theirs = att_x[step - 1, half : 2 * half, :]
+            term_part[step - 1] = dot_tn(theirs, w_far[...].reshape(half, quarter)).astype(BF16)
+            src, dst = term_part.at[step - 1], far_term.at[:, columns(x_at)]
+            gathers[15].append(send(src, dst, gather_send.at[15, i], gather_recv.at[15, i], x_to(step)))
 
     row = lax.broadcasted_iota(jnp.int32, (SEQ, SEQ), 0)
     col = lax.broadcasted_iota(jnp.int32, (SEQ, SEQ), 1)
@@ -168,8 +225,9 @@
     def head(ref, rows, base, h):
         return ref[rows, base + h * HDIM : base + (h + 1) * HDIM]
 
-    def forward(s):
+    def forward_norm(s):
         rows = slice(s * SEQ, (s + 1) * SEQ)
+        own_norm = own_ret if s == 0 else away_ret
 
         def normalise(i, carry):
             at = pl.multiple_of(s * SEQ + i * 16, 16)
@@ -179,12 +237,16 @@
             own_norm[pl.ds(pl.multiple_of(i * 16, 16), 16), :] = (chunk * scale).astype(BF16)
             return carry
 
-        own_norm = own_ret if s == 0 else away_ret
         lax.fori_loop(0, SEQ // 16, normalise, 0)
         for c in range(4):
             flipped = own_norm[:, c * quarter : (c + 1) * quarter].T
-            norm_t[2 * c : 2 * c + 2, :, :, rows] = flipped.reshape((2,) + norm_t.shape[1:3] + (SEQ,))
-        gather_norm(s)
+            tall = norm_t.shape[3]
+            for k in range(8):
+                norm_t[s, k % 4, 2 * c + k // 4] = flipped[k * tall : (k + 1) * tall, :]
+
+    def forward(s):
+        rows = slice(s * SEQ, (s + 1) * SEQ)
+        own_norm = own_ret if s == 0 else away_ret
         for c in range(3):
             cols = slice(c * half, (c + 1) * half)
             qkv[rows, cols] = dot_nn(own_norm[...], w_in[:, cols]).astype(BF16)
@@ -199,21 +261,22 @@
                 pair.append(dot_nn(p.astype(BF16), head(qkv, rows, 2 * half, hh)).astype(BF16))
             both = jnp.concatenate(pair, axis=1)
             g_att[rows, h * HDIM : (h + 2) * HDIM] = both
-        att_t[:, rows] = g_att[rows, :].T
-        gather_att(s)
-        term = own_term if s == 0 else away_term
-        for c in range(features // wide):
-            cols = slice(c * wide, (c + 1) * wide)
-            term[:, cols] = dot_nn(g_att[rows, :], w_out[:, cols]).astype(BF16)
+        if s == 0:
+            att_t[0:half, :] = g_att[rows, :].T
+            for c in range(features // wide):
+                cols = slice(c * wide, (c + 1) * wide)
+                own_term[:, cols] = dot_nn(g_att[rows, :], w_out[:, cols]).astype(BF16)
 
     def backward_heads(s):
         rows = slice(s * SEQ, (s + 1) * SEQ)
-        g_att[rows, :] = dot_nt(gs[rows, :], w_out[...]).astype(BF16)
+        if s == 0:
+            g_att[rows, :] = dot_nt(gs[...], w_out[...]).astype(BF16)
+        grad_ref = g_att if s == 0 else far_grad_in
         for h in range(0, heads, 2):
             g_q, g_k, g_v = [], [], []
             for hh in (h, h + 1):
                 p = prob[s * heads + hh]
-                ga = head(g_att, rows, 0, hh)
+                ga = head(grad_ref, slice(0, SEQ), 0, hh)
                 g_prob = dot_nt(ga, head(qkv, rows, 2 * half, hh))
                 inner = jnp.sum(p * g_prob, axis=-1, keepdims=True)
                 g_score = (p * (g_prob - inner) * inv_sqrt).astype(BF16)
@@ -221,17 +284,17 @@
                 g_k.append(dot_tn(g_score, head(qkv, rows, 0, hh)).astype(BF16))
                 g_v.append(dot_tn(p.astype(BF16), ga).astype(BF16))
             for c, pieces in enumerate((g_q, g_k, g_v)):
-                base = c * half + h * HDIM
-                g_qkv[rows, base : base + 2 * HDIM] = jnp.concatenate(pieces, axis=1)
-        for c in (2, 0, 1):
-            gather_grad(s, c)
+                g_qkv[c, rows, h * HDIM : (h + 2) * HDIM] = jnp.concatenate(pieces, axis=1)
 
     def backward_input(s):
         rows = slice(s * SEQ, (s + 1) * SEQ)
         wide = min(512, features)
         for c in range(features // wide):
             cols = slice(c * wide, (c + 1) * wide)
-            g_norm[:, cols] = dot_nt(g_qkv[rows, :], w_in[cols, :])
+            acc = dot_nt(g_qkv[0, rows, :], w_in[cols, 0:half])
+            for p in (1, 2):
+                acc = acc + dot_nt(g_qkv[p, rows, :], w_in[cols, p * half : (p + 1) * half])
+            g_norm[:, cols] = acc
         result = own_ret if s == 0 else away_ret
 
         def returned(i, carry):
@@ -283,92 +346,158 @@
         copy(near[t].at[0, 1 - z_at], last[t], t, 6, z_mate)
 
     def weight_grad(t, c):
-        cols = slice(c * half, (c + 1) * half)
+        tall = (quarter // 4, SEQ)
+
+        def norm_rows(pair, i):
+            return jnp.concatenate([pair(s)[2 * i : 2 * i + 2].reshape(tall) for s in range(2)], axis=1)
+
         for i in range(X_SIZE):
-            tall = (quarter // 4, 2 * SEQ)
-            acc = dot_nn(norm_t[2 * i : 2 * i + 2, y_at].reshape(tall), g_qkv[:, cols])
+            acc = dot_nn(norm_rows(lambda s: norm_t.at[s, y_at], i), g_qkv[c])
             for j in range(3):
-                acc = acc + dot_nn(norm_y[j, 2 * i : 2 * i + 2].reshape(tall), grad_y[j, :, cols])
+                acc = acc + dot_nn(norm_rows(lambda s: norm_y.at[j, s], i), grad_y[j, c])
             parts[t][i] = acc.astype(BF16).reshape(parts[t].shape[1:])
 
-    def out_weight_grad():
+    def out_weight_grad(t, slot):
         block = half // X_SIZE
-        mine = gs[:, pl.ds(pl.multiple_of(x_at * quarter, quarter), quarter)]
+        mine = gs[:, columns(x_at)]
         for i in range(X_SIZE):
-            rows = slice(i * block, (i + 1) * block)
+            rows = slice(slot * half + i * block, slot * half + (i + 1) * block)
             acc = dot_nn(att_t[rows, :], mine)
             for j in range(3):
                 acc = acc + dot_nn(att_x[j, rows, :], g_x[j])
-            parts[0][i] = acc.astype(BF16).reshape(parts[0].shape[1:])
-
-    for load in loads:
+            parts[t][i] = acc.astype(BF16).reshape(parts[t].shape[1:])
+
+    def out_spread(t, pieces, joined):
+        msgs[t, 6].wait_recv()
+        pieces[...] = total(near[t][0, z_at], last[t][...]).astype(pieces.dtype)
+        joined[:, columns(x_at)] = pieces[x_at]
+        for i, step in enumerate(STEPS):
+            src, dst = pieces.at[lax.rem(x_at + step, 4)], joined.at[:, columns(x_at)]
+            msgs[t, 7 + i] = send(src, dst, ring_send.at[t, 7 + i], ring_recv.at[t, 7 + i], x_to(step))
+
+    def out_joined(t):
+        for i in range(3):
+            msgs[t, 7 + i].wait_recv()
+
+    def add_up(out, base, one, two):
+        def body(i, carry):
+            at = pl.ds(pl.multiple_of(i * 16, 16), 16)
+            out[at, :] = total(base[at, :], one[at, :], two[at, :]).astype(BF16)
+            return carry
+
+        lax.fori_loop(0, SEQ // 16, body, 0)
+
+    loads[1].wait()
+    gather_out_grad()
+    far_pair()
+    rest = SEQ - head_rows
+    x_moves.append(to_mirror(x_in.at[pl.ds(head_rows, rest), :], xs.at[pl.ds(SEQ + head_rows, rest), :], 6))
+    loads[0].wait()
+    forward_norm(0)
+    far_spread()
+    gather_norm(0)
+    for load in loads[2:]:
         load.wait()
-    gather_out_grad(0)
     forward(0)
+    gather_att(0)
     backward_heads(0)
+    for c in (2, 0, 1):
+        gather_grad(0, c)
+    far_grad_parts()
     backward_input(0)
-
-    x_move.wait_recv()
+    far_move = far_grad_sum()
+
+    for move in x_moves:
+        move.wait_recv()
+    forward_norm(1)
+    gather_norm(1)
     forward(1)
-    term_move = to_mirror(away_term, back_term, 2)
-    g_move.wait_recv()
-    gather_out_grad(1)
+    att_move = to_mirror(g_att.at[second], far_att, 3)
+    for c in (2, 0, 1):
+        relay_grad(0, c)
+    far_move.wait_recv()
     backward_heads(1)
+    for c in (2, 0, 1):
+        gather_grad(1, c)
     backward_input(1)
-    ret_move = to_mirror(away_ret, back_ret, 3)
-    arrived(2, 3, 4, 5)
-    out_weight_grad()
+    ret_move = to_mirror(away_ret, back_ret, 4)
+
+    arrived(2)
+    out_weight_grad(0, 0)
     ring_start(0)
+    att_move.wait_recv()
+    att_t[half : 2 * half, :] = far_att[...].T
+    gather_att(1)
+    relay_grad(1, 2)
+    arrived(3)
+    out_weight_grad(4, 1)
+    relay_grad(1, 0)
+    ring_start(4)
+    far_term_parts()
+    relay_grad(1, 1)
+    ring_forward(0)
     arrived(0, 1, 8, 11)
     weight_grad(1, 2)
     ring_start(1)
-    ring_forward(0)
     arrived(6, 9)
     weight_grad(2, 0)
     ring_start(2)
+    ring_forward(4)
     ring_forward(1)
     arrived(7, 10)
     weight_grad(3, 1)
     ring_start(3)
     ring_finish(0)
+    ring_finish(4)
     ring_forward(2)
     ring_finish(1)
     ring_forward(3)
-    msgs[0, 6].wait_recv()
-    out_sum[...] = total(near[0][0, z_at], last[0][...])
-    spread = [
-        send(out_sum.at[lax.rem(x_at + step, 4)], out_recv.at[3 - step], ring_send.at[0, 7 + i], ring_recv.at[0, 7 + i], x_to(step))
-        for i, step in enumerate(STEPS)
-    ]
-
-    def add_up(out, base, one, two):
-        def body(i, carry):
-            at = pl.ds(pl.multiple_of(i * 16, 16), 16)
-            out[at, :] = total(base[at, :], one[at, :], two[at, :]).astype(BF16)
-            return carry
-
-        lax.fori_loop(0, SEQ // 16, body, 0)
-
-    term_move.wait_recv()
-    add_up(hidden_out, xs, own_term, back_term)
+    arrived(15)
+    add_up(hidden_out, xs, own_term, far_term)
+    out_spread(4, out_cast, out_far)
+    out_spread(0, out_sum, out_own)
     ring_finish(2)
+    out_joined(4)
+    out_move = to_mirror(out_far, out_back, 5)
     ring_finish(3)
     ret_move.wait_recv()
     add_up(grad_in, gs, own_ret, back_ret)
-    for i, step in enumerate(STEPS):
-        spread[i].wait_recv()
-
-    def out_columns(at):
-        return pl.ds(pl.multiple_of(at * quarter, quarter), quarter)
-
-    dwo_out[:, out_columns(x_at)] = out_sum[x_at]
-    for r in (1, 2, 3):
-        dwo_out[:, out_columns(lax.rem(x_at + r, 4))] = out_recv[r - 1]
     for t in (1, 2, 3):
         msgs[t, 6].wait_recv()
         outs[t][...] = total(near[t][0, z_at], last[t][...])
+    out_joined(0)
+    out_move.wait_recv()
+    dwo_out[...] = total(out_own[...], out_back[...])
     for made in started:
         made.wait_send()
+
+
+def hand_on_kernel(*refs):
+    count = 6
+    srcs, dsts, bufs = refs[:count], refs[count : 2 * count], refs[2 * count : 3 * count]
+    in_sem, out_sem = refs[3 * count :]
+    ins = [pltpu.make_async_copy(srcs[i], bufs[i], in_sem.at[i]) for i in range(count)]
+    outs = [pltpu.make_async_copy(bufs[i], dsts[i], out_sem.at[i]) for i in range(count)]
+    for move in ins:
+        move.start()
+    for i in range(count):
+        ins[i].wait()
+        outs[i].start()
+    for move in outs:
+        move.wait()
+
+
+def hand_on(arrays):
+    anywhere = pl.BlockSpec(memory_space=pl.ANY)
+    return pl.pallas_call(
+        hand_on_kernel,
+        out_shape=tuple(jax.ShapeDtypeStruct(a.shape, a.dtype) for a in arrays),
+        in_specs=[anywhere] * 6,
+        out_specs=(anywhere,) * 6,
+        scratch_shapes=[pltpu.VMEM(a.shape, a.dtype) for a in arrays]
+        + [pltpu.SemaphoreType.DMA((6,)), pltpu.SemaphoreType.DMA((6,))],
+        name="hand_on",
+    )(*arrays)
 
 
 def on_device(hidden_in, grad_out, w_query, w_key, w_value, w_out, pattern):
@@ -379,41 +508,57 @@
     ranks = X_SIZE * Z_SIZE * Y_SIZE
     tails = [(half // ranks, features)] + [(features // ranks, half)] * 3
     both, one = (2 * SEQ, features), (SEQ, features)
+    quarter = features // 4
+    small = (half // ranks, quarter)
     scratch = [
         pltpu.VMEM(both, BF16),
-        pltpu.VMEM(both, BF16),
+        pltpu.VMEM(one, BF16),
         pltpu.VMEM((features, 3 * half), BF16),
         pltpu.VMEM((half, features), BF16),
-        pltpu.VMEM((8, 4, features // ranks, 2 * SEQ), BF16),
-        pltpu.VMEM((half, 2 * SEQ), BF16),
+        pltpu.VMEM((Z_SIZE, Y_SIZE, half // 8, quarter), BF16),
+        pltpu.VMEM((2, 4, 8, features // ranks, SEQ), BF16),
+        pltpu.VMEM((2 * half, SEQ), BF16),
         pltpu.VMEM((2 * SEQ, 3 * half), BF16),
         pltpu.VMEM((2 * heads, SEQ, SEQ), F32),
         pltpu.VMEM((2 * SEQ, half), BF16),
-        pltpu.VMEM((2 * SEQ, 3 * half), BF16),
+        pltpu.VMEM((3, 2 * SEQ, half), BF16),
         pltpu.VMEM((2 * SEQ, 128), F32),
         pltpu.VMEM(one, F32),
-    ] + [pltpu.VMEM(one, BF16)] * 6
-    quarter = features // 4
-    small = (half // ranks, quarter)
+    ] + [pltpu.VMEM(one, BF16)] * 5
+    scratch += [pltpu.VMEM((SEQ, half), BF16)] * 3
     scratch += [
-        pltpu.VMEM((3, 8, features // ranks, 2 * SEQ), BF16),
-        pltpu.VMEM((3, 2 * SEQ, 3 * half), BF16),
-        pltpu.VMEM((3, half, 2 * SEQ), BF16),
-        pltpu.VMEM((3, 2 * SEQ, quarter), BF16),
+        pltpu.VMEM((SEQ, half), F32),
+        pltpu.VMEM((3, SEQ, half), BF16),
+        pltpu.VMEM((3, SEQ, half), BF16),
+        pltpu.VMEM((3, SEQ, quarter), BF16),
+    ]
+    scratch += [
+        pltpu.VMEM((3, 2, 8, features // ranks, SEQ), BF16),
+        pltpu.VMEM((3, 3, 2 * SEQ, half), BF16),
+        pltpu.VMEM((3, 2 * half, SEQ), BF16),
+        pltpu.VMEM((3, SEQ, quarter), BF16),
         pltpu.VMEM((4,) + small, F32),
-        pltpu.VMEM((3,) + small, F32),
-        pltpu.VMEM((X_SIZE, Z_SIZE, Y_SIZE) + small, BF16),
-    ] + [pltpu.VMEM((X_SIZE, Z_SIZE) + tails[1], BF16)] * 3
+        pltpu.VMEM((4,) + small, BF16),
+        pltpu.VMEM(tails[0], F32),
+        pltpu.VMEM(tails[0], BF16),
+        pltpu.VMEM(tails[0], BF16),
+    ]
+    lead = (X_SIZE, Z_SIZE)
+    scratch += (
+        [pltpu.VMEM(lead + (Y_SIZE,) + small, BF16)]
+        + [pltpu.VMEM(lead + tails[1], BF16)] * 3
+        + [pltpu.VMEM(lead + (Y_SIZE,) + small, BF16)]
+    )
     for lead in ((2,), (2, 2), ()):
-        scratch += [pltpu.VMEM(lead + tail, BF16) for tail in [(4,) + small] + tails[1:]]
+        scratch += [pltpu.VMEM(lead + tail, BF16) for tail in [(4,) + small] + tails[1:] + [(4,) + small]]
     scratch += [
         pltpu.SemaphoreType.DMA((6,)),
-        pltpu.SemaphoreType.DMA((4,)),
-        pltpu.SemaphoreType.DMA((4,)),
-        pltpu.SemaphoreType.DMA((4, 10)),
-        pltpu.SemaphoreType.DMA((4, 10)),
-        pltpu.SemaphoreType.DMA((12, 3)),
-        pltpu.SemaphoreType.DMA((12, 3)),
+        pltpu.SemaphoreType.DMA((7,)),
+        pltpu.SemaphoreType.DMA((7,)),
+        pltpu.SemaphoreType.DMA((5, 10)),
+        pltpu.SemaphoreType.DMA((5, 10)),
+        pltpu.SemaphoreType.DMA((16, 4)),
+        pltpu.SemaphoreType.DMA((16, 4)),
     ]
     outs = pl.pallas_call(
         sublayer_kernel,
@@ -427,6 +572,7 @@
         ),
         name="sublayer",
     )(pattern, hidden_in, grad_out, w_query[0], w_key[0], w_value[0], w_out[0])
+    outs = hand_on(outs)
     return (outs[0], outs[1]) + tuple(out[None] for out in outs[2:])
 
 

time: 120 us -> 99.1 us (0.83)
  Pallas kernels: 113 us -> 98.1 us
  local copies, waits for them, and re-layouts: 6.46 us -> 0 us
    pallas_call x1, Pallas kernels: 113 us -> 95.9 us  [on_device(): pl.pallas_call(sublayer_kernel, out_shape=(jax.ShapeDtypeStruct(one, BF16...]
    unnamed x14 -> x0, local copies, waits for them, and re-layouts: 6.46 us -> none
    pallas_call x0 -> x1, Pallas kernels: none -> 2.28 us  [hand_on(): pl.pallas_call(hand_on_kernel, out_shape=tuple((jax.ShapeDtypeStruct(a.sh...]
where the time goes in v4:
time: 99.1 us; the launch traced here: 98.9 us
  Pallas kernels  98.1 us (99%)
    pallas_call x1, Pallas kernels, on_device(): pl.pallas_call(sublayer_kernel, out_shape=(jax.ShapeDtypeStruct(one, BF16...  95.9 us
    pallas_call x1, Pallas kernels, hand_on(): pl.pallas_call(hand_on_kernel, out_shape=tuple((jax.ShapeDtypeStruct(a.sh...  2.28 us

profile of v4, /device:TPU:1, one launch (start us, length us, event | category | flops | bytes accessed | tf_op | source)
XLA Modules:
  0.0 98.9 jit_solution(6431158092919936291)
XLA Ops:
  0.6 95.9 %sublayer.1 = (bf16[128,2048]{1,0:T(8,128)(2,1)}, bf16[128,2048]{1,0:T(8,128)(2,1)}, f32[64,512]{1,0:T(8,128)}, f32[64,512]{1,0:T(8,128)}, f32[64,512]{1,0:T(8,128)}, /*index=5*/f32[16,2048]{1,0:T(8,128)}) custom-call(s32[4,3]{1,0:T(4,128)} %refs_0_.1, bf16[128,2048]{1,0:T(8,128)(2,1)} %refs_1_.1, bf16[128,2048]{1,0:T(8,128)(2,1)} %refs_2_.1, ...), custom_call_target="tpu_custom_call" | custom-call | tf_op jit(solution)/shard_map/sublayer/pallas_call | solution.py:563
  96.5 2.3 %hand_on.1 = (bf16[128,2048]{1,0:T(8,128)(2,1)}, bf16[128,2048]{1,0:T(8,128)(2,1)}, f32[64,512]{1,0:T(8,128)}, f32[64,512]{1,0:T(8,128)}, f32[64,512]{1,0:T(8,128)}, /*index=5*/f32[16,2048]{1,0:T(8,128)}) custom-call(bf16[128,2048]{1,0:T(8,128)(2,1)} %get-tuple-element.18.refs_0_, bf16[128,2048]{1,0:T(8,128)(2,1)} %get-tuple-element.19.refs_1_, ...), custom_call_target="tpu_custom_call" | custom-call | tf_op jit(solution)/shard_map/hand_on/pallas_call | solution.py:492

commit v5 on v4

--- a/solution.py
+++ b/solution.py
@@ -422,44 +422,44 @@
     backward_input(1)
     ret_move = to_mirror(away_ret, back_ret, 4)
 
-    arrived(2)
-    out_weight_grad(0, 0)
-    ring_start(0)
     att_move.wait_recv()
     att_t[half : 2 * half, :] = far_att[...].T
     gather_att(1)
+    arrived(2)
+    out_weight_grad(0, 0)
     relay_grad(1, 2)
+    relay_grad(1, 0)
     arrived(3)
     out_weight_grad(4, 1)
-    relay_grad(1, 0)
+    relay_grad(1, 1)
+    ring_start(0)
     ring_start(4)
-    far_term_parts()
-    relay_grad(1, 1)
-    ring_forward(0)
     arrived(0, 1, 8, 11)
     weight_grad(1, 2)
     ring_start(1)
     arrived(6, 9)
     weight_grad(2, 0)
     ring_start(2)
-    ring_forward(4)
     ring_forward(1)
     arrived(7, 10)
     weight_grad(3, 1)
     ring_start(3)
+    far_term_parts()
+    ring_forward(0)
+    ring_forward(4)
+    ring_forward(2)
     ring_finish(0)
     ring_finish(4)
-    ring_forward(2)
+    ring_forward(3)
     ring_finish(1)
-    ring_forward(3)
-    arrived(15)
-    add_up(hidden_out, xs, own_term, far_term)
     out_spread(4, out_cast, out_far)
     out_spread(0, out_sum, out_own)
     ring_finish(2)
     out_joined(4)
     out_move = to_mirror(out_far, out_back, 5)
     ring_finish(3)
+    arrived(15)
+    add_up(hidden_out, xs, own_term, far_term)
     ret_move.wait_recv()
     add_up(grad_in, gs, own_ret, back_ret)
     for t in (1, 2, 3):

time: 99.1 us -> 99.3 us (level)
  no operation moved by 1% of the time
where the time goes in v5:
time: 99.3 us; the launch traced here: 99.1 us
  Pallas kernels  98.3 us (99%)
    pallas_call x1, Pallas kernels, on_device(): pl.pallas_call(sublayer_kernel, out_shape=(jax.ShapeDtypeStruct(one, BF16...  96.1 us
    pallas_call x1, Pallas kernels, hand_on(): pl.pallas_call(hand_on_kernel, out_shape=tuple((jax.ShapeDtypeStruct(a.sh...  2.28 us

profile of v5, /device:TPU:1, one launch (start us, length us, event | category | flops | bytes accessed | tf_op | source)
XLA Modules:
  0.0 99.1 jit_solution(9207168610086266434)
XLA Ops:
  0.6 96.1 %sublayer.1 = (bf16[128,2048]{1,0:T(8,128)(2,1)}, bf16[128,2048]{1,0:T(8,128)(2,1)}, f32[64,512]{1,0:T(8,128)}, f32[64,512]{1,0:T(8,128)}, f32[64,512]{1,0:T(8,128)}, /*index=5*/f32[16,2048]{1,0:T(8,128)}) custom-call(s32[4,3]{1,0:T(4,128)} %refs_0_.1, bf16[128,2048]{1,0:T(8,128)(2,1)} %refs_1_.1, bf16[128,2048]{1,0:T(8,128)(2,1)} %refs_2_.1, ...), custom_call_target="tpu_custom_call" | custom-call | tf_op jit(solution)/shard_map/sublayer/pallas_call | solution.py:563
  96.7 2.3 %hand_on.1 = (bf16[128,2048]{1,0:T(8,128)(2,1)}, bf16[128,2048]{1,0:T(8,128)(2,1)}, f32[64,512]{1,0:T(8,128)}, f32[64,512]{1,0:T(8,128)}, f32[64,512]{1,0:T(8,128)}, /*index=5*/f32[16,2048]{1,0:T(8,128)}) custom-call(bf16[128,2048]{1,0:T(8,128)(2,1)} %get-tuple-element.18.refs_0_, bf16[128,2048]{1,0:T(8,128)(2,1)} %get-tuple-element.19.refs_1_, ...), custom_call_target="tpu_custom_call" | custom-call | tf_op jit(solution)/shard_map/hand_on/pallas_call | solution.py:492
